TPU v7x, 32 devices: a whole 2x2x4 slice. The times are simulated.
32 devices in a mesh: dp: 8 (over y, x, core), expert: 4 (over z).
Axes of the slice: x: 2, y: 2, z: 4, core: 2. Of those that a mesh axis runs over, the one named last changes fastest.
Arguments:
- tokens: bfloat16 [32, 512, 1536], P(('dp', 'expert')), may hold values from -6 to 6
- seq_lengths: int32 [32], P(('dp', 'expert')), may hold values from 256 to 512, as said below
- routes: int32 [32, 512, 8], P(('dp', 'expert')), may hold values from 0 to 19, all different within a row
- norm_attn: bfloat16 [1536], P('expert'), may hold values from 0.5 to 1.5
- query_key_value_weight: bfloat16 [1536, 2560], P('expert'), may hold values from -0.15625 to 0.15625
- w_out: bfloat16 [1536, 1536], P('expert'), may hold values from -1.5 to 1.5
- norm_moe: bfloat16 [1536], P('expert'), may hold values from 0.5 to 1.5
- router: bfloat16 [1536, 20], P('expert'), may hold values from -0.078125 to 0.078125
- expert_in: bfloat16 [20, 1536, 1024], P('expert', 'dp'), may hold values from -0.15625 to 0.15625
- expert_out: bfloat16 [20, 512, 1536], P('expert', 'dp'), may hold values from -1 to 1
- cotangent: bfloat16 [32, 512, 1536], P(('dp', 'expert')), may hold values from -6 to 6
Outputs:
- output: bfloat16 [32, 512, 1536], P(('dp', 'expert'))
- grad_tokens: bfloat16 [32, 512, 1536], P(('dp', 'expert'))
- grad_norm_attn: float32 [1536], P('expert')
- grad_w_qkv: float32 [1536, 2560], P('expert')
- grad_w_out: float32 [1536, 1536], P('expert')
- grad_norm_moe: float32 [1536], P('expert')
- grad_router: float32 [1536, 20], P('expert')
- grad_expert_in: float32 [20, 1536, 1024], P('expert', 'dp')
- grad_expert_out: float32 [20, 512, 1536], P('expert', 'dp')
Inputs may be any that keep to these rules, and one draw needn't show every extreme that they name: `seq_lengths`: the first sequence is full.
All inputs are finite; a program needn't handle non-finite values.
Results may differ from a plain program's by a relative error of at most 0.02.
Values may be sent and summed in bfloat16 or wider, within the bound.
A program may use at most 320 MiB of HBM per device.

v0:
```python
import math

import jax
import jax.numpy as jnp
from jax import lax
from jax.sharding import PartitionSpec as P

QUERY_HEADS = 24
KEY_VALUE_HEADS = 8
HEAD_SIZE = 64
TOPK = 8


PRECISE = lax.Precision.HIGHEST
EPSILON = 1e-06
MASKED = -1000000000.0


def tables(length, head):
    half_width = head // 2
    frequency = jnp.exp(
        jnp.arange(half_width, dtype=jnp.float32) * (-math.log(10000.0) / half_width)
    )
    angles = jnp.arange(length, dtype=jnp.float32)[:, None] * frequency[None, :]
    return (jnp.cos(angles), jnp.sin(angles))


def rotate(value_rows, cosine, sine_table):
    half_width = value_rows.shape[-1] // 2
    front_half = value_rows[..., :half_width]
    back_half = value_rows[..., half_width:]
    return jnp.concatenate(
        [
            front_half * cosine - back_half * sine_table,
            back_half * cosine + front_half * sine_table,
        ],
        -1,
    )


def unrotate(value_rows, cosine, sine_table):
    half_width = value_rows.shape[-1] // 2
    front_half = value_rows[..., :half_width]
    back_half = value_rows[..., half_width:]
    return jnp.concatenate(
        [
            front_half * cosine + back_half * sine_table,
            back_half * cosine - front_half * sine_table,
        ],
        -1,
    )


def norm_apply(value_rows, gain_vec):
    factor = lax.rsqrt(jnp.mean(value_rows * value_rows, -1, keepdims=True) + EPSILON)
    return (value_rows * factor * gain_vec, factor)


def norm_back(value_rows, factor, gain_vec, incoming):
    unit_rows = value_rows * factor
    scaled = incoming * gain_vec
    gain_grad = jnp.sum((incoming * unit_rows).reshape(-1, value_rows.shape[-1]), 0)
    return (
        factor * (scaled - unit_rows * jnp.mean(scaled * unit_rows, -1, keepdims=True)),
        gain_grad,
    )


def masked_scores(query_rows, key_rows_all, length, scale_factor):
    sequence_length = query_rows.shape[0]
    scores = (
        jnp.einsum("qgrh,kgh->grqk", query_rows, key_rows_all, preferred_element_type=jnp.float32)
        * scale_factor
    )
    position = jnp.arange(sequence_length)
    allowed = (position[None, :] <= position[:, None]) & (position[None, :] < length)
    return jnp.where(allowed, scores, MASKED)


def attend_forward(member, scale_factor):
    query_rows, key_rows_all, value_rows, length = member
    scores = masked_scores(query_rows, key_rows_all, length, scale_factor)
    topmost = jnp.max(scores, -1, keepdims=True)
    exponent = jnp.exp(scores - topmost)
    totals = jnp.sum(exponent, -1, keepdims=True)
    weights = (exponent / totals).astype(jnp.bfloat16)
    mixed_heads = jnp.einsum(
        "grqk,kgh->qgrh", weights, value_rows, preferred_element_type=jnp.float32
    )
    return (
        mixed_heads.astype(jnp.bfloat16).reshape(query_rows.shape[0], -1),
        topmost + jnp.log(totals),
    )


def attend_backward(member, scale_factor):
    query_rows, key_rows_all, value_rows, length, log_total, upstream = member
    scores = masked_scores(query_rows, key_rows_all, length, scale_factor)
    weights = jnp.exp(scores - log_total)
    upstream_heads = upstream.reshape(query_rows.shape)
    weight_grad = jnp.einsum(
        "qgrh,kgh->grqk", upstream_heads, value_rows, preferred_element_type=jnp.float32
    )
    score_grad = (
        weights * (weight_grad - jnp.sum(weights * weight_grad, -1, keepdims=True))
    ).astype(jnp.bfloat16)
    query_grad = (
        jnp.einsum("grqk,kgh->qgrh", score_grad, key_rows_all, preferred_element_type=jnp.float32)
        * scale_factor
    )
    key_grad = (
        jnp.einsum("grqk,qgrh->kgh", score_grad, query_rows, preferred_element_type=jnp.float32)
        * scale_factor
    )
    value_grad = jnp.einsum(
        "grqk,qgrh->kgh",
        weights.astype(jnp.bfloat16),
        upstream_heads,
        preferred_element_type=jnp.float32,
    )
    return (query_grad, key_grad, value_grad)


def per_device(
    tokens,
    seq_lengths,
    routes,
    norm_attn,
    query_key_value_weight,
    w_out,
    norm_moe,
    router,
    expert_in,
    expert_out,
    cotangent,
):
    qkv_full, out_full, gain_one, gain_two, router_full = (
        lax.all_gather(query_key_value_weight, "expert", axis=0, tiled=True),
        lax.all_gather(w_out, "expert", axis=0, tiled=True),
        lax.all_gather(norm_attn, "expert", axis=0, tiled=True),
        lax.all_gather(norm_moe, "expert", axis=0, tiled=True),
        lax.all_gather(router, "expert", axis=0, tiled=True),
    )
    sequences_per_shard, sequence_length, model_width = tokens.shape
    query_groups = QUERY_HEADS // KEY_VALUE_HEADS
    owners = lax.axis_size("expert")
    local_experts = expert_in.shape[0]
    experts_all = local_experts * owners
    capacity = sequences_per_shard * sequence_length * TOPK // experts_all
    slot_count = experts_all * capacity
    scale_factor = HEAD_SIZE ** (-0.5)
    inputs = tokens.astype(jnp.float32)
    gain_first = gain_one.astype(jnp.float32)
    gain_second = gain_two.astype(jnp.float32)
    normed_first, factor_first = norm_apply(inputs, gain_first)
    normed_low = normed_first.astype(jnp.bfloat16)
    projected_rows = jnp.einsum(
        "std,df->stf", normed_low, qkv_full, preferred_element_type=jnp.float32
    )
    cosine, sine_table = tables(sequence_length, HEAD_SIZE)
    query_unrotated = projected_rows[..., : QUERY_HEADS * HEAD_SIZE].reshape(
        sequences_per_shard, sequence_length, KEY_VALUE_HEADS, query_groups, HEAD_SIZE
    )
    key_unrotated = projected_rows[
        ..., QUERY_HEADS * HEAD_SIZE : (QUERY_HEADS + KEY_VALUE_HEADS) * HEAD_SIZE
    ].reshape(sequences_per_shard, sequence_length, KEY_VALUE_HEADS, HEAD_SIZE)
    value_unrotated = projected_rows[..., (QUERY_HEADS + KEY_VALUE_HEADS) * HEAD_SIZE :].reshape(
        sequences_per_shard, sequence_length, KEY_VALUE_HEADS, HEAD_SIZE
    )
    cos_five = cosine[None, :, None, None, :]
    sin_five = sine_table[None, :, None, None, :]
    cos_four = cosine[None, :, None, :]
    sin_four = sine_table[None, :, None, :]
    query_rows = rotate(query_unrotated, cos_five, sin_five).astype(jnp.bfloat16)
    key_rows_all = rotate(key_unrotated, cos_four, sin_four).astype(jnp.bfloat16)
    value_rows = value_unrotated.astype(jnp.bfloat16)
    attended, log_total = lax.map(
        lambda member: attend_forward(member, scale_factor),
        (query_rows, key_rows_all, value_rows, seq_lengths),
    )
    attn_proj = jnp.einsum("sti,id->std", attended, out_full, preferred_element_type=jnp.float32)
    hidden_sum = inputs + attn_proj
    normed_second, factor_second = norm_apply(hidden_sum, gain_second)
    second_low = normed_second.astype(jnp.bfloat16).reshape(-1, model_width)
    router_wide = router_full.astype(jnp.float32)
    logits = jnp.dot(second_low.astype(jnp.float32), router_wide, precision=PRECISE)
    flat_routes = routes.reshape(-1, TOPK)
    picked = jnp.take_along_axis(logits, flat_routes, 1)
    exponent = jnp.exp(picked - jnp.max(picked, -1, keepdims=True))
    gating = exponent / jnp.sum(exponent, -1, keepdims=True)
    position = jnp.arange(sequence_length)
    live_tokens = position[None, :] < seq_lengths[:, None]
    live_pairs = jnp.broadcast_to(live_tokens[:, :, None], routes.shape).reshape(-1)
    chosen = flat_routes.reshape(-1)
    onehot = (chosen[:, None] == jnp.arange(experts_all)[None, :]) & live_pairs[:, None]
    counts = onehot.astype(jnp.int32)
    ranking = jnp.sum((jnp.cumsum(counts, 0) - counts) * counts, -1)
    kept_pairs = live_pairs & (ranking < capacity)
    slot_index = jnp.where(kept_pairs, chosen * capacity + ranking, slot_count)
    pair_token = jnp.arange(chosen.shape[0], dtype=jnp.int32) // TOPK
    slot_token = jnp.zeros((slot_count + 1,), jnp.int32).at[slot_index].set(pair_token)[:slot_count]
    slot_live = jnp.zeros((slot_count + 1,), jnp.bool_).at[slot_index].set(kept_pairs)[:slot_count]
    kept_gate = gating.reshape(-1) * kept_pairs.astype(jnp.float32)
    slot_weight = (
        jnp.zeros((slot_count + 1,), jnp.float32).at[slot_index].set(kept_gate)[:slot_count]
    )
    send_rows = jnp.where(slot_live[:, None], second_low[slot_token], jnp.zeros((), jnp.bfloat16))
    received = lax.all_to_all(
        send_rows.reshape(owners, local_experts * capacity, model_width),
        "expert",
        split_axis=0,
        concat_axis=0,
        tiled=True,
    ).reshape(owners, local_experts, capacity, model_width)
    inner_full, down_full = (
        lax.all_gather(expert_in, "dp", axis=1, tiled=True),
        lax.all_gather(expert_out, "dp", axis=1, tiled=True),
    )
    hidden_width = down_full.shape[1]
    gate_up = jnp.einsum("secd,edf->secf", received, inner_full, preferred_element_type=jnp.float32)
    gate_part = gate_up[..., :hidden_width]
    up_part = gate_up[..., hidden_width:]
    sigmoid_part = jax.nn.sigmoid(gate_part)
    activated = gate_part * sigmoid_part
    hidden_low = (activated * up_part).astype(jnp.bfloat16)
    expert_rows = jnp.einsum(
        "sech,ehd->secd", hidden_low, down_full, preferred_element_type=jnp.float32
    ).astype(jnp.bfloat16)
    returned = lax.all_to_all(
        expert_rows.reshape(owners, local_experts * capacity, model_width),
        "expert",
        split_axis=0,
        concat_axis=0,
        tiled=True,
    ).reshape(slot_count, model_width)
    padded_rows = jnp.concatenate([returned, jnp.zeros((1, model_width), jnp.bfloat16)], 0)
    pair_rows = padded_rows[slot_index].reshape(-1, TOPK, model_width)
    kept_weight = kept_gate.reshape(-1, TOPK)
    mixture = jnp.einsum("tk,tkd->td", kept_weight, pair_rows, precision=PRECISE)
    live_rows = live_tokens.reshape(-1, 1).astype(jnp.float32)
    combined = live_rows * (hidden_sum.reshape(-1, model_width) + mixture)
    output = combined.astype(jnp.bfloat16).reshape(tokens.shape)
    upstream = cotangent.astype(jnp.float32).reshape(-1, model_width) * live_rows
    gate_grad = kept_pairs.reshape(-1, TOPK).astype(jnp.float32) * jnp.einsum(
        "tkd,td->tk", pair_rows, upstream, precision=PRECISE
    )
    picked_grad = gating * (gate_grad - jnp.sum(gating * gate_grad, -1, keepdims=True))
    route_onehot = (flat_routes[:, :, None] == jnp.arange(experts_all)[None, None, :]).astype(
        jnp.float32
    )
    logit_grad = jnp.einsum("tk,tke->te", picked_grad, route_onehot, precision=PRECISE)
    grad_send = jnp.where(
        slot_live[:, None], slot_weight[:, None] * upstream[slot_token], 0.0
    ).astype(jnp.bfloat16)
    grad_received = lax.all_to_all(
        grad_send.reshape(owners, local_experts * capacity, model_width),
        "expert",
        split_axis=0,
        concat_axis=0,
        tiled=True,
    ).reshape(owners, local_experts, capacity, model_width)
    inner_full, down_full = (
        lax.all_gather(expert_in, "dp", axis=1, tiled=True),
        lax.all_gather(expert_out, "dp", axis=1, tiled=True),
    )
    hidden_grad = jnp.einsum(
        "secd,ehd->sech", grad_received, down_full, preferred_element_type=jnp.float32
    )
    gate_part_grad = hidden_grad * up_part * sigmoid_part * (1.0 + gate_part * (1.0 - sigmoid_part))
    up_grad = hidden_grad * activated
    gate_up_grad = jnp.concatenate([gate_part_grad, up_grad], -1).astype(jnp.bfloat16)
    row_grad = jnp.einsum(
        "secf,edf->secd", gate_up_grad, inner_full, preferred_element_type=jnp.float32
    ).astype(jnp.bfloat16)
    row_back = lax.all_to_all(
        row_grad.reshape(owners, local_experts * capacity, model_width),
        "expert",
        split_axis=0,
        concat_axis=0,
        tiled=True,
    ).reshape(slot_count, model_width)
    down_weight_grad = jnp.einsum(
        "sech,secd->ehd", hidden_low, grad_received, preferred_element_type=jnp.float32
    )
    inner_weight_grad = jnp.einsum(
        "secd,secf->edf", received, gate_up_grad, preferred_element_type=jnp.float32
    )
    inner_sum, down_sum = (
        lax.psum_scatter(
            inner_weight_grad.astype(jnp.bfloat16), "dp", scatter_dimension=1, tiled=True
        ).astype(jnp.float32),
        lax.psum_scatter(
            down_weight_grad.astype(jnp.bfloat16), "dp", scatter_dimension=1, tiled=True
        ).astype(jnp.float32),
    )
    padded_back = jnp.concatenate([row_back, jnp.zeros((1, model_width), jnp.bfloat16)], 0)
    pair_back = padded_back[slot_index].reshape(-1, TOPK, model_width)
    second_grad = jnp.sum(pair_back.astype(jnp.float32), 1) + jnp.dot(
        logit_grad, router_wide.T, precision=PRECISE
    )
    router_grad = jnp.dot(second_low.astype(jnp.float32).T, logit_grad, precision=PRECISE)
    hidden_back, gain_two_grad = norm_back(
        hidden_sum, factor_second, gain_second, second_grad.reshape(hidden_sum.shape)
    )
    total_grad = upstream.reshape(hidden_sum.shape) + hidden_back
    total_low = total_grad.astype(jnp.bfloat16)
    out_weight_grad = jnp.einsum(
        "sti,std->id", attended, total_low, preferred_element_type=jnp.float32
    )
    attended_grad = jnp.einsum(
        "std,id->sti", total_low, out_full, preferred_element_type=jnp.float32
    ).astype(jnp.bfloat16)
    query_grad, key_grad, value_grad = lax.map(
        lambda member: attend_backward(member, scale_factor),
        (query_rows, key_rows_all, value_rows, seq_lengths, log_total, attended_grad),
    )
    query_grad = unrotate(query_grad, cos_five, sin_five)
    key_grad = unrotate(key_grad, cos_four, sin_four)
    projected_grad = jnp.concatenate(
        [
            query_grad.reshape(sequences_per_shard, sequence_length, -1),
            key_grad.reshape(sequences_per_shard, sequence_length, -1),
            value_grad.reshape(sequences_per_shard, sequence_length, -1),
        ],
        -1,
    ).astype(jnp.bfloat16)
    qkv_weight_grad = jnp.einsum(
        "std,stf->df", normed_low, projected_grad, preferred_element_type=jnp.float32
    )
    first_grad = jnp.einsum(
        "stf,df->std", projected_grad, qkv_full, preferred_element_type=jnp.float32
    )
    input_back, gain_one_grad = norm_back(inputs, factor_first, gain_first, first_grad)
    input_grad = (total_grad + input_back).astype(jnp.bfloat16)
    shards = (
        lax.psum_scatter(
            qkv_weight_grad.astype(jnp.bfloat16), "expert", scatter_dimension=0, tiled=True
        ).astype(jnp.float32),
        lax.psum_scatter(
            out_weight_grad.astype(jnp.bfloat16), "expert", scatter_dimension=0, tiled=True
        ).astype(jnp.float32),
        lax.psum_scatter(
            gain_one_grad.astype(jnp.bfloat16), "expert", scatter_dimension=0, tiled=True
        ).astype(jnp.float32),
        lax.psum_scatter(
            gain_two_grad.astype(jnp.bfloat16), "expert", scatter_dimension=0, tiled=True
        ).astype(jnp.float32),
        lax.psum_scatter(
            router_grad.astype(jnp.bfloat16), "expert", scatter_dimension=0, tiled=True
        ).astype(jnp.float32),
    )
    summed = (
        lax.psum(shards[0].astype(jnp.bfloat16), "dp").astype(jnp.float32),
        lax.psum(shards[1].astype(jnp.bfloat16), "dp").astype(jnp.float32),
        lax.psum(shards[2].astype(jnp.bfloat16), "dp").astype(jnp.float32),
        lax.psum(shards[3].astype(jnp.bfloat16), "dp").astype(jnp.float32),
        lax.psum(shards[4].astype(jnp.bfloat16), "dp").astype(jnp.float32),
    )
    return (
        output,
        input_grad,
        summed[2],
        summed[0],
        summed[1],
        summed[3],
        summed[4],
        inner_sum,
        down_sum,
    )


def solution(mesh):
    return jax.shard_map(
        per_device,
        mesh=mesh,
        in_specs=(
            P(("dp", "expert"), None, None),
            P(("dp", "expert")),
            P(("dp", "expert"), None, None),
            P("expert"),
            P("expert", None),
            P("expert", None),
            P("expert"),
            P("expert", None),
            P("expert", "dp", None),
            P("expert", "dp", None),
            P(("dp", "expert"), None, None),
        ),
        out_specs=(
            P(("dp", "expert"), None, None),
            P(("dp", "expert"), None, None),
            P("expert"),
            P("expert", None),
            P("expert", None),
            P("expert"),
            P("expert", None),
            P("expert", "dp", None),
            P("expert", "dp", None),
        ),
        check_vma=False,
    )
```

profile of v0, /device:TPU:0, one launch (start us, length us, event | category | flops | bytes accessed | tf_op | source)
XLA Modules:
  0.0 2128.6 jit_solution(7163580515706601558)
XLA Ops:
  11.5 13.6 all-gather
  27.1 13.4 all-gather.1
  41.1 20.9 all_gather.27
  70.6 15.5 scatter_custom_fusion.1
  90.3 21.0 gather_fusion.2
  111.4 20.9 gather.28
  132.2 22.4 %all-gather.7.cloned.1.call-done = bf16[1536,2560]{1,0:T(8,128)(2,1)} async-done(((bf16[384,2560]{1,0:T(8,128)(2,1)}), bf16[1536,2560]{1,0:T(8,128)(2,1)}) %all-gather.7.cloned.1.call-update) | async-done | bytes 7864336 | tf_op jit(solution)/shard_map/all_gather | solution.py:138
  209.9 34.0 %all-gather.9.cloned.1.call-done = bf16[1536,1536]{1,0:T(8,128)(2,1)} async-done(((bf16[384,1536]{1,0:T(8,128)(2,1)}), bf16[1536,1536]{1,0:T(8,128)(2,1)}) %all-gather.9.cloned.1.call-update) | async-done | bytes 4718608 | tf_op jit(solution)/shard_map/all_gather | solution.py:139
  252.0 33.0 %gather_fusion.4 = f32[4096]{0:T(1024)S(1)} fusion(f32[512,20]{0,1:T(8,128)S(1)} %fusion.119, s32[4096]{0:T(1024)S(1)} %copy-done.2), kind=kCustom, calls=%fused_computation.4 | custom fusion | bytes 65536 | tf_op jit(solution)/shard_map/jit(take_along_axis)/gather | solution.py:188
  287.4 15.7 scatter_custom_fusion.2
  303.1 17.7 scatter_custom_fusion
  321.0 13.7 select_convert_fusion
  341.1 19.2 gather_fusion
  384.4 229.9 %all-to-all-done.2 = bf16[4,1020,1536]{2,1,0:T(8,128)(2,1)} async-done(((bf16[4,1020,1536]{2,1,0:T(8,128)(2,1)}), bf16[4,1020,1536]{2,1,0:T(8,128)(2,1)}, u32[]{:S(2)}, u32[]{:S(2)}) %all-to-all-start.2) | async-done | bytes 12533792 | tf_op jit(solution)/shard_map/all_to_all | solution.py:255
  631.4 262.1 %all-to-all-done = bf16[4,1020,1536]{2,1,0:T(8,128)(2,1)} async-done(((bf16[4,1020,1536]{2,1,0:T(8,128)(2,1)}), bf16[4,1020,1536]{2,1,0:T(8,128)(2,1)}, u32[]{:S(2)}, u32[]{:S(2)}) %all-to-all-start) | async-done | bytes 12533792 | tf_op jit(solution)/shard_map/all_to_all | solution.py:208
  903.3 24.1 %fusion.33 = f32[4,5,204,1024]{3,2,0,1:T(8,128)} fusion(bf16[5,1536,1024]{2,1,0:T(8,128)(2,1)} %all-gather.11.cloned.1.call-done, bf16[4,5,204,1536]{3,2,1,0:T(8,128)(2,1)} %reshape.515), kind=kOutput, calls=%fused_computation.58 | convolution fusion | flops 12834570240 | bytes 44974080 | tf_op jit(solution)/shard_map/secd,edf->secf/dot_general | solution.py:220
  927.4 21.9 %fusion.27 = (bf16[4,5,204,512]{3,2,0,1:T(8,128)(2,1)}, bf16[4,5,204,512]{3,2,0,1:T(8,128)(2,1)}, bf16[4,5,204,512]{3,2,0,1:T(8,128)(2,1)}) fusion(f32[4,5,204,1024]{3,2,0,1:T(8,128)} %fusion.33, bf16[5,512,1536]{2,1,0:T(8,128)(2,1)} %all-gather.13.cloned.1.call-done, bf16[4,5,204,1536]{3,2,1,0:T(8,128)(2,1)} %reshape.521), kind=kOutput, calls=%fused_computation.49 | convolution fusion | flops 6448619520 | bytes 49643520 | tf_op jit(solution)/shard_map/secd,ehd->sech/dot_general | solution.py:266
  949.3 24.9 %convert_bitcast_fusion = bf16[4,5,204,1536]{3,2,0,1:T(8,128)(2,1)} fusion(bf16[5,1536,1024]{2,1,0:T(8,128)(2,1)} %all-gather.11.cloned.1.call-done, bf16[4,5,204,512]{3,2,0,1:T(8,128)(2,1)} %get-tuple-element.77, bf16[4,5,204,512]{3,2,0,1:T(8,128)(2,1)} %get-tuple-element.76), kind=kOutput, calls=%fused_computation.28 | convolution fusion | flops 12857548800 | bytes 36618240 | tf_op jit(solution)/shard_map/secf,edf->secd/dot_general | solution.py:272
  1027.2 246.4 %all-to-all-done.3 = bf16[4,1020,1536]{2,1,0:T(8,128)(2,1)} async-done(((bf16[4,1020,1536]{2,1,0:T(8,128)(2,1)}), bf16[4,1020,1536]{2,1,0:T(8,128)(2,1)}, u32[]{:S(2)}, u32[]{:S(2)}) %all-to-all-start.3) | async-done | bytes 12533792 | tf_op jit(solution)/shard_map/all_to_all | solution.py:275
  1279.9 15.7 bitcast_convert_fusion.1
  1297.6 15.1 reshape.523
  1323.9 228.6 %all-to-all-done.1 = bf16[4,1020,1536]{2,1,0:T(8,128)(2,1)} async-done(((bf16[4,1020,1536]{2,1,0:T(8,128)(2,1)}), bf16[4,1020,1536]{2,1,0:T(8,128)(2,1)}, u32[]{:S(2)}, u32[]{:S(2)}) %all-to-all-start.1) | async-done | bytes 12533792 | tf_op jit(solution)/shard_map/all_to_all | solution.py:229
  1576.2 31.5 %gather_fusion.3 = bf16[4096,1536]{1,0:T(8,128)(2,1)} fusion(bf16[4081,1536]{1,0:T(8,128)(2,1)} %concatenate.62, s32[4096]{0:T(1024)S(1)} %broadcast_clamp_fusion), kind=kCustom, calls=%fused_computation.3 | custom fusion | bytes 25182208 | tf_op jit(solution)/shard_map/gather | solution.py:297
  1607.6 31.5 %gather_fusion.1 = bf16[4096,1536]{1,0:T(8,128)(2,1)} fusion(bf16[4081,1536]{1,0:T(8,128)(2,1)} %concatenate.60, s32[4096]{0:T(1024)S(1)} %broadcast_clamp_fusion), kind=kCustom, calls=%fused_computation.1 | custom fusion | bytes 25182208 | tf_op jit(solution)/shard_map/gather | solution.py:237
  1639.2 25.1 %fusion.12 = f32[512,1,8]{2,1,0:T(1,128)S(1)} fusion(bf16[4096,1536]{1,0:T(8,128)(2,1)} %gather_fusion.1, f32[512,1536,1]{1,0,2:T(8,128)} %get-tuple-element.84), kind=kOutput, calls=%fused_computation.31 | convolution fusion | flops 75497472 | bytes 15745024 | tf_op jit(solution)/shard_map/tkd,td->tk/dot_general | solution.py:244
  1692.2 21.4 %fusion = (f32[8,3,512]{2,1,0:T(4,128)S(1)}, f32[8,512,512,3]{2,1,3,0:T(8,128)}) fusion(f32[8,3,512]{2,1,0:T(4,128)S(1)} %log_add_fusion, f32[8,512,512,3]{2,1,3,0:T(8,128)} %get-tuple-element.94, pred[512,512]{0,1:T(8,128)(4,1)S(1)} %copy-done.18, bf16[512,8,64,1]{0,2,3,1:T(8,128)(2,1)} %bitcast.271, bf16[512,8,3,64]{0,3,2,1:T(8,128)(2,1)S(1)} %bitcast.267), kind=kOutput, calls=%fused_computation.12 | convolution fusion | flops 836751360 | bytes 52789248 | tf_op jit(solution)/shard_map/while/body/eval_jaxpr/qgrh,kgh->grqk/dot_general | solution.py:101
  1713.6 22.4 %fusion.2 = bf16[8,3,512,512]{2,3,1,0:T(8,128)(2,1)} fusion(f32[8,512,512,3]{2,1,3,0:T(8,128)} %get-tuple-element.99, f32[8,3,512]{2,1,0:T(4,128)S(1)} %get-tuple-element.98, f32[8,3,512]{2,1,0:T(4,128)S(1)} %log_add_fusion, f32[8,512,512,3]{2,1,3,0:T(8,128)} %get-tuple-element.94, pred[512,512]{0,1:T(8,128)(4,1)S(1)} %copy-done.18), kind=kLoop, calls=%fused_computation.14 | loop fusion | flops 37748736 | bytes 63275008 | tf_op jit(solution)/shard_map/while/body/eval_jaxpr/convert_element_type | solution.py:106
  1777.2 25.7 %bitcast_convert_fusion = bf16[5,1536,1024]{2,1,0:T(8,128)(2,1)} fusion(bf16[4,5,204,1536]{3,2,1,0:T(8,128)(2,1)} %reshape.515, bf16[4,5,204,512]{3,2,0,1:T(8,128)(2,1)} %get-tuple-element.77, bf16[4,5,204,512]{3,2,0,1:T(8,128)(2,1)} %get-tuple-element.76), kind=kOutput, calls=%fused_computation.8 | convolution fusion | flops 12859146240 | bytes 36618240 | tf_op jit(solution)/shard_map/secd,secf->edf/dot_general | solution.py:285
  1830.7 79.3 %reduce-scatter.8.cloned.1.call-done = bf16[384,2560]{1,0:T(8,128)(2,1)} async-done(((bf16[1536,2560]{1,0:T(8,128)(2,1)}), bf16[384,2560]{1,0:T(8,128)(2,1)}) %reduce-scatter.8.cloned.1.call-update) | async-done | bytes 1966096 | tf_op jit(solution)/shard_map/reduce_scatter | solution.py:336
  1934.7 22.4 %all-reduce.4 = (bf16[384]{0:T(512)(128)(2,1)S(1)}, bf16[384]{0:T(512)(128)(2,1)S(1)}, bf16[384,20]{0,1:T(8,128)(2,1)S(1)}) all-reduce(bf16[384]{0:T(512)(128)(2,1)S(1)} %dynamic-slice.2, bf16[384]{0:T(512)(128)(2,1)S(1)} %dynamic-slice.4, bf16[384,20]{0,1:T(8,128)(2,1)S(1)} %copy.114), channel_id=1, replica_groups=mesh['dp'=8,'expert'=4] {'dp'}, use_global_device_ids=true, to_apply=%region_19.20 | all-reduce | flops 8448 | bytes 33792 | tf_op jit(solution)/shard_map/psum | solution.py:355
  1958.8 84.2 %reduce-scatter.12.cloned.1.call-done = bf16[5,192,1024]{2,1,0:T(8,128)(2,1)} async-done(((bf16[5,1536,1024]{2,1,0:T(8,128)(2,1)}), bf16[5,192,1024]{2,1,0:T(8,128)(2,1)}) %reduce-scatter.12.cloned.1.call-update) | async-done | bytes 1966096 | tf_op jit(solution)/shard_map/reduce_scatter | solution.py:289
  2046.9 68.7 %all-reduce.9.cloned.1.call-done = (bf16[384,2560]{1,0:T(8,128)(2,1)}, bf16[384,1536]{1,0:T(8,128)(2,1)}) async-done(((bf16[384,2560]{1,0:T(8,128)(2,1)}, bf16[384,1536]{1,0:T(8,128)(2,1)}), (bf16[384,2560]{1,0:T(8,128)(2,1)}, bf16[384,1536]{1,0:T(8,128)(2,1)})) %all-reduce.9.cloned.1.call-update) | async-done | bytes 3145744 | tf_op jit(solution)/shard_map/psum | solution.py:353
  (326 shorter events, 369.5 us)
Async XLA Ops:
  7.2 33.9 %copy-start.70 = (bf16[384,20]{0,1:T(8,128)(2,1)S(1)}, bf16[384,20]{0,1:T(8,128)(2,1)}, u32[]{:S(2)}) copy-start(bf16[384,20]{0,1:T(8,128)(2,1)} %param.18) | copy-start | bytes 46084
  7.2 147.4 %all-gather.7.cloned.1.call-start = ((), (), s32[]{:S(2)}) async-start(), calls=%async_computation.9 | async-start | bytes 9830400 | tf_op jit(solution)/shard_map/all_gather | solution.py:138
  8.0 235.9 %all-gather.9.cloned.1.call-start = ((), (), s32[]{:S(2)}) async-start(), calls=%async_computation.10 | async-start | bytes 5898240 | tf_op jit(solution)/shard_map/all_gather | solution.py:139
  8.7 894.5 %all-gather.11.cloned.1.call-start = ((), (), s32[]{:S(2)}) async-start(), calls=%async_computation.11 | async-start | bytes 17694720 | tf_op jit(solution)/shard_map/all_gather | solution.py:216
  9.6 76.5 %copy-start.8 = (s32[1,512,8]{2,1,0:T(8,128)}, s32[1,512,8]{2,1,0:T(8,128)S(1)}, u32[]{:S(2)}) copy-start(s32[1,512,8]{2,1,0:T(8,128)S(1)} %copy.77) | copy-start | bytes 49156
  9.9 76.2 %copy-start.50 = (s32[4096]{0:T(1024)}, s32[4096]{0:T(1024)S(1)}, u32[]{:S(2)}) copy-start(s32[4096]{0:T(1024)S(1)} %eq.38) | copy-start | bytes 49156
  10.8 185.8 %copy-start.17 = (pred[512,512]{0,1:T(8,128)(4,1)}, pred[512,512]{0,1:T(8,128)(4,1)S(1)}, u32[]{:S(2)}) copy-start(pred[512,512]{0,1:T(8,128)(4,1)S(1)} %fusion.75) | copy-start | bytes 786436
  11.3 59.2 %copy-start.58 = (pred[4096]{0:T(1024)(128)(4,1)}, pred[4096]{0:T(1024)(128)(4,1)S(1)}, u32[]{:S(2)}) copy-start(pred[4096]{0:T(1024)(128)(4,1)S(1)} %broadcast_in_dim.144) | copy-start | bytes 12292
  27.1 144.6 %copy-start.27 = (f32[512,32]{0,1:T(8,128)}, f32[512,32]{0,1:T(8,128)S(1)}, u32[]{:S(2)}) copy-start(f32[512,32]{0,1:T(8,128)S(1)} %get-tuple-element.91) | copy-start | bytes 196612
  27.1 144.6 %copy-start.29 = (f32[512,32]{0,1:T(8,128)}, f32[512,32]{0,1:T(8,128)S(1)}, u32[]{:S(2)}) copy-start(f32[512,32]{0,1:T(8,128)S(1)} %get-tuple-element.92) | copy-start | bytes 196612
  111.3 43.3 %copy-start.13 = (bf16[1,512,1536]{2,1,0:T(8,128)(2,1)S(1)}, bf16[1,512,1536]{2,1,0:T(8,128)(2,1)}, u32[]{:S(2)}) copy-start(bf16[1,512,1536]{2,1,0:T(8,128)(2,1)} %param.11) | copy-start | bytes 4718596
  111.3 43.3 %copy-start.64 = (f32[1536]{0:T(1024)S(1)}, f32[1536]{0:T(1024)}, u32[]{:S(2)}) copy-start(f32[1536]{0:T(1024)} %reshape.597) | copy-start | bytes 18436
  111.3 43.3 %copy-start.74 = (f32[512]{0:T(512)S(1)}, f32[512]{0:T(512)}, u32[]{:S(2)}) copy-start(f32[512]{0:T(512)} %add_rsqrt_fusion.1) | copy-start | bytes 6148
  196.6 47.3 %copy-start.14 = (bf16[1,512,1536]{2,1,0:T(8,128)(2,1)S(1)}, bf16[1,512,1536]{2,1,0:T(8,128)(2,1)}, u32[]{:S(2)}) copy-start(bf16[1,512,1536]{2,1,0:T(8,128)(2,1)} %param.11) | copy-start | bytes 4718596
  251.4 89.7 %copy-start = (bf16[512,1536]{1,0:T(8,128)(2,1)}, bf16[512,1536]{1,0:T(8,128)(2,1)S(1)}, u32[]{:S(2)}) copy-start(bf16[512,1536]{1,0:T(8,128)(2,1)S(1)} %fusion.61) | copy-start | bytes 4718596
  251.9 34.8 %copy-start.51 = (s32[4096]{0:T(1024)S(1)}, s32[4096]{0:T(1024)}, u32[]{:S(2)}) copy-start(s32[4096]{0:T(1024)} %copy-done.50) | copy-start | bytes 49156
  252.0 34.8 %copy-start.53 = (s32[4096]{0:T(1024)S(1)}, s32[4096]{0:T(1024)}, u32[]{:S(2)}) copy-start(s32[4096]{0:T(1024)} %copy-done.52) | copy-start | bytes 49156
  252.0 34.8 %copy-start.59 = (pred[4096]{0:T(1024)(128)(4,1)S(1)}, pred[4096]{0:T(1024)(128)(4,1)}, u32[]{:S(2)}) copy-start(pred[4096]{0:T(1024)(128)(4,1)} %copy-done.58) | copy-start | bytes 12292
  285.2 49.5 %copy-start.20 = (f32[512,8]{1,0:T(8,128)}, f32[512,8]{1,0:T(8,128)S(1)}, u32[]{:S(2)}) copy-start(f32[512,8]{1,0:T(8,128)S(1)} %reshape.563) | copy-start | bytes 49156
  285.4 49.3 %copy-start.60 = (f32[512]{0:T(512)}, f32[512]{0:T(512)S(1)}, u32[]{:S(2)}) copy-start(f32[512]{0:T(512)S(1)} %fusion.117) | copy-start | bytes 6148
  334.7 279.6 %all-to-all-start.2 = ((bf16[4,1020,1536]{2,1,0:T(8,128)(2,1)}), bf16[4,1020,1536]{2,1,0:T(8,128)(2,1)}, u32[]{:S(2)}, u32[]{:S(2)}) async-start(bf16[4,1020,1536]{2,1,0:T(8,128)(2,1)} %select_convert_fusion), calls=%async_computation.2 | async-start | bytes 25165824 | tf_op jit(solution)/shard_map/all_to_all | solution.py:255
  614.3 279.2 %all-to-all-start = ((bf16[4,1020,1536]{2,1,0:T(8,128)(2,1)}), bf16[4,1020,1536]{2,1,0:T(8,128)(2,1)}, u32[]{:S(2)}, u32[]{:S(2)}) async-start(bf16[4,1020,1536]{2,1,0:T(8,128)(2,1)} %broadcast_select_fusion), calls=%async_computation | async-start | bytes 25165824 | tf_op jit(solution)/shard_map/all_to_all | solution.py:208
  621.0 306.4 %all-gather.13.cloned.1.call-start = ((), (), s32[]{:S(2)}) async-start(), calls=%async_computation.12 | async-start | bytes 8847360 | tf_op jit(solution)/shard_map/all_gather | solution.py:217
  994.8 278.8 %all-to-all-start.3 = ((bf16[4,1020,1536]{2,1,0:T(8,128)(2,1)}), bf16[4,1020,1536]{2,1,0:T(8,128)(2,1)}, u32[]{:S(2)}, u32[]{:S(2)}) async-start(bf16[4,1020,1536]{2,1,0:T(8,128)(2,1)} %reshape.522), calls=%async_computation.3 | async-start | bytes 25165824 | tf_op jit(solution)/shard_map/all_to_all | solution.py:275
  1273.6 278.8 %all-to-all-start.1 = ((bf16[4,1020,1536]{2,1,0:T(8,128)(2,1)}), bf16[4,1020,1536]{2,1,0:T(8,128)(2,1)}, u32[]{:S(2)}, u32[]{:S(2)}) async-start(bf16[4,1020,1536]{2,1,0:T(8,128)(2,1)} %reshape.516), calls=%async_computation.1 | async-start | bytes 25165824 | tf_op jit(solution)/shard_map/all_to_all | solution.py:229
  1279.9 524.9 %reduce-scatter.14.cloned.1.call-start = ((), (), s32[]{:S(2)}) async-start(), calls=%async_computation.16 | async-start | bytes 8847360 | tf_op jit(solution)/shard_map/reduce_scatter | solution.py:292
  1295.7 535.0 %reduce-scatter.10.cloned.1.call-start = ((), (), s32[]{:S(2)}) async-start(), calls=%async_computation.14 | async-start | bytes 5898240 | tf_op jit(solution)/shard_map/reduce_scatter | solution.py:339
  1684.1 225.9 %reduce-scatter.8.cloned.1.call-start = ((), (), s32[]{:S(2)}) async-start(), calls=%async_computation.13 | async-start | bytes 9830400 | tf_op jit(solution)/shard_map/reduce_scatter | solution.py:336
  1774.0 159.7 %reduce-scatter.16.cloned.1.call-start = ((), (), s32[]{:S(2)}) async-start(), calls=%async_computation.17 | async-start | bytes 491520
  1777.2 265.9 %reduce-scatter.12.cloned.1.call-start = ((), (), s32[]{:S(2)}) async-start(), calls=%async_computation.15 | async-start | bytes 17694720 | tf_op jit(solution)/shard_map/reduce_scatter | solution.py:289
  1802.9 312.7 %all-reduce.9.cloned.1.call-start = ((), (), s32[]{:S(2)}) async-start(), calls=%async_computation.18 | async-start | bytes 6291456 | tf_op jit(solution)/shard_map/psum | solution.py:353
  1830.7 90.8 %copy-start.5 = (f32[1,512,1536]{2,1,0:T(8,128)S(1)}, f32[1,512,1536]{2,1,0:T(8,128)}, u32[]{:S(2)}) copy-start(f32[1,512,1536]{2,1,0:T(8,128)} %copy-done.3) | copy-start | bytes 9437188
  (69 other events, 733.8 us)
Sparse Core Ops, SparseCore 0:
  9.6 144.9 all-gather.6
  156.2 87.6 all-gather.8
  245.8 83.7 all-gather.10
  623.4 53.3 all-gather.12
  1295.9 70.5 reduce-scatter.13
  1684.2 84.3 reduce-scatter.9
  1774.1 135.8 reduce-scatter.7
  1912.3 21.3 reduce-scatter.15
  1937.2 105.7 reduce-scatter.11
  2046.2 69.3 all-reduce.8
where the time goes:
time: 2130 us
  waiting for transfers between devices  1260 us (59%)
  local copies, waits for them, and re-layouts  353 us (17%)
  matrix products  282 us (13%)
  other arithmetic  104 us (5%)
  blocking collectives  81.5 us (4%)
  starting transfers between devices  26.5 us (1%)
    all_to_all x1, waiting for transfers between devices, per_device(): lax.all_to_all(send_rows.reshape(owners, local_experts * capacity, model_...  262 us
    all_to_all x1, waiting for transfers between devices, per_device(): lax.all_to_all(row_grad.reshape(owners, local_experts * capacity, model_w...  246 us
    all_to_all x1, waiting for transfers between devices, per_device(): lax.all_to_all(grad_send.reshape(owners, local_experts * capacity, model_...  230 us
    all_to_all x1, waiting for transfers between devices, per_device(): lax.all_to_all(expert_rows.reshape(owners, local_experts * capacity, mode...  229 us
    reduce_scatter x1, waiting for transfers between devices, per_device(): lax.psum_scatter(inner_weight_grad.astype(jnp.bfloat16), 'dp', scatter_di...  84.2 us
    reduce_scatter x1, waiting for transfers between devices, per_device(): lax.psum_scatter(qkv_weight_grad.astype(jnp.bfloat16), 'expert', scatter_...  79.3 us
    psum x1, waiting for transfers between devices, per_device(): lax.psum(shards[0].astype(jnp.bfloat16), 'dp').astype(jnp.float32)  68.7 us
  transfers between devices with their start and end apart: 14, of which 10 were waited for; matrix products, arithmetic and copies ran while one was open for 31% of the time, Pallas kernels for 0%

commit v1 on v0

v1 whole, which is shorter than its diff:
```python
import math

import jax
import jax.numpy as jnp
from jax import lax
from jax.experimental import pallas as pl
from jax.experimental.pallas import tpu as pltpu
from jax.sharding import PartitionSpec as P

QUERY_HEADS = 24
KEY_VALUE_HEADS = 8
HEAD_SIZE = 64
TOPK = 8
AUX = 128

PRECISE = lax.Precision.HIGHEST
EPSILON = 1e-06
MASKED = -1000000000.0
F32 = jnp.float32
BF16 = jnp.bfloat16


def tables(length, head):
    half_width = head // 2
    frequency = jnp.exp(jnp.arange(half_width, dtype=F32) * (-math.log(10000.0) / half_width))
    angles = jnp.arange(length, dtype=F32)[:, None] * frequency[None, :]
    return (jnp.cos(angles), jnp.sin(angles))


def rotate(value_rows, cosine, sine_table):
    half_width = value_rows.shape[-1] // 2
    front_half = value_rows[..., :half_width]
    back_half = value_rows[..., half_width:]
    return jnp.concatenate(
        [
            front_half * cosine - back_half * sine_table,
            back_half * cosine + front_half * sine_table,
        ],
        -1,
    )


def norm_apply(value_rows, gain_vec):
    factor = lax.rsqrt(jnp.mean(value_rows * value_rows, -1, keepdims=True) + EPSILON)
    return (value_rows * factor * gain_vec, factor)


def norm_back(value_rows, factor, gain_vec, incoming):
    unit_rows = value_rows * factor
    scaled = incoming * gain_vec
    gain_grad = jnp.sum(incoming * unit_rows, 0)
    return (
        factor * (scaled - unit_rows * jnp.mean(scaled * unit_rows, -1, keepdims=True)),
        gain_grad,
    )


def dot(spec, a, b):
    return jnp.einsum(spec, a, b, preferred_element_type=F32)


def masked_scores(query_rows, key_rows_all, length, scale_factor):
    sequence_length = query_rows.shape[0]
    scores = dot("qgrh,kgh->grqk", query_rows, key_rows_all) * scale_factor
    position = jnp.arange(sequence_length)
    allowed = (position[None, :] <= position[:, None]) & (position[None, :] < length)
    return jnp.where(allowed, scores, MASKED)


def attend_forward(query_rows, key_rows_all, value_rows, length, scale_factor):
    scores = masked_scores(query_rows, key_rows_all, length, scale_factor)
    topmost = jnp.max(scores, -1, keepdims=True)
    exponent = jnp.exp(scores - topmost)
    totals = jnp.sum(exponent, -1, keepdims=True)
    weights = (exponent / totals).astype(BF16)
    mixed_heads = dot("grqk,kgh->qgrh", weights, value_rows)
    return (
        mixed_heads.astype(BF16).reshape(query_rows.shape[0], -1),
        topmost + jnp.log(totals),
    )


def attend_backward(query_rows, key_rows_all, value_rows, length, log_total, upstream, scale_factor):
    scores = masked_scores(query_rows, key_rows_all, length, scale_factor)
    weights = jnp.exp(scores - log_total)
    upstream_heads = upstream.reshape(query_rows.shape)
    weight_grad = dot("qgrh,kgh->grqk", upstream_heads, value_rows)
    score_grad = (
        weights * (weight_grad - jnp.sum(weights * weight_grad, -1, keepdims=True))
    ).astype(BF16)
    query_grad = dot("grqk,kgh->qgrh", score_grad, key_rows_all) * scale_factor
    key_grad = dot("grqk,qgrh->kgh", score_grad, query_rows) * scale_factor
    value_grad = dot("grqk,qgrh->kgh", weights.astype(BF16), upstream_heads)
    return (query_grad, key_grad, value_grad)


def split_two(values):
    high = values.astype(BF16)
    low = (values - high.astype(F32)).astype(BF16)
    return (high, low)


MESH = pl.DeviceIdType.MESH
VMEM_LIMIT = 60 * 1024 * 1024


def vmem_spec():
    return pl.BlockSpec(memory_space=pltpu.VMEM)


def any_spec():
    return pl.BlockSpec(memory_space=pl.ANY)


def kernel_params(collective):
    return pltpu.CompilerParams(
        collective_id=collective, has_side_effects=True, vmem_limit_bytes=VMEM_LIMIT
    )


def greet_all(me, owners, dp_index, bits):
    barrier = pltpu.get_barrier_semaphore()
    for bit in range(bits):
        pl.semaphore_signal(
            barrier, inc=1, device_id={"dp": partner_of(dp_index, bit)}, device_id_type=MESH
        )
    ends = (me > 0, me < owners - 1)
    for offset, there in zip((-1, 1), ends):

        @pl.when(there)
        def _():
            pl.semaphore_signal(
                barrier, inc=1, device_id={"expert": me + offset}, device_id_type=MESH
            )

    pl.semaphore_wait(barrier, bits + ends[0].astype(jnp.int32) + ends[1].astype(jnp.int32))


def bit_of(index, bit):
    return lax.rem(index // (1 << bit), 2)


def partner_of(index, bit):
    return index + (1 - 2 * bit_of(index, bit)) * (1 << bit)


def line_sends(me, owners, source_of, target_of, send, recv, slot):
    first = []
    for side in range(2):
        toward = 1 - 2 * side
        behind = me if side == 0 else owners - 1 - me

        def copy(step, side=side, toward=toward):
            origin = me - toward * step
            return pltpu.make_async_remote_copy(
                src_ref=source_of(step, origin),
                dst_ref=target_of(origin),
                send_sem=send.at[slot, side, step],
                recv_sem=recv.at[slot, side, step],
                device_id={"expert": me + toward},
                device_id_type=MESH,
            )

        first.append((behind, copy))
    return first


def line_step(step, sides, owners):
    for behind, copy in sides:
        if step > 0:

            @pl.when(behind >= step)
            def _():
                copy(step - 1).wait_recv()

        if step < owners - 1:

            @pl.when((behind >= step) & (behind < owners - 1))
            def _():
                copy(step).start()


def line_finish(sides, owners):
    for behind, copy in sides:
        for step in range(owners - 1):

            @pl.when((behind >= step) & (behind < owners - 1))
            def _():
                copy(step).wait_send()


def line_gather(blocks, owners, collective):
    count = len(blocks)

    def kernel(*refs):
        own, outs = refs[:count], refs[count : 2 * count]
        send, recv, local = refs[2 * count :]
        me = lax.axis_index("expert")
        greet_all(me, owners, 0, 0)
        lines, copies = [], []
        for i in range(count):

            def source_of(step, origin, i=i):
                return own[i] if step == 0 else outs[i].at[origin]

            def target_of(origin, i=i):
                return outs[i].at[origin]

            lines.append(line_sends(me, owners, source_of, target_of, send, recv, i))
        for step in range(owners):
            for i in range(count):
                line_step(step, lines[i], owners)
            if step == 0:
                for i in range(count):
                    copies.append(pltpu.make_async_copy(own[i], outs[i].at[me], local.at[i]))
                    copies[-1].start()
        for i in range(count):
            copies[i].wait()
            line_finish(lines[i], owners)

    return pl.pallas_call(
        kernel,
        out_shape=[jax.ShapeDtypeStruct((owners,) + b.shape, b.dtype) for b in blocks],
        in_specs=[vmem_spec()] * count,
        out_specs=[any_spec()] * count,
        scratch_shapes=[
            pltpu.SemaphoreType.DMA((count, 2, owners - 1)),
            pltpu.SemaphoreType.DMA((count, 2, owners - 1)),
            pltpu.SemaphoreType.DMA((count,)),
        ],
        compiler_params=kernel_params(collective),
    )(*blocks)


def add_rows(target, addend, chunk):
    @pl.loop(0, target.shape[0] // chunk)
    def _(index):
        rows = pl.ds(pl.multiple_of(index * chunk, chunk), chunk)
        target[rows, :] = (target[rows, :].astype(F32) + addend[rows, :].astype(F32)).astype(
            target.dtype
        )


def scatter_line(own, held, out, send, recv, me, owners, chunk):
    def copy(side, step, source):
        toward = 1 - 2 * side
        return pltpu.make_async_remote_copy(
            src_ref=source,
            dst_ref=held.at[side, step],
            send_sem=send.at[side, step],
            recv_sem=recv.at[side, step],
            device_id={"expert": me + toward},
            device_id_type=MESH,
        )

    def advance(step):
        for side in range(2):
            toward = 1 - 2 * side
            behind = me if side == 0 else owners - 1 - me
            block = own.at[me + toward * (owners - 1 - step)]

            @pl.when(behind == 0)
            def _():
                copy(side, step, block).start()

            if step > 0:
                before = held.at[side, step - 1]

                @pl.when((behind >= 1) & (behind <= step))
                def _():
                    copy(side, step - 1, before).wait_recv()
                    add_rows(before, block, chunk)
                    copy(side, step, before).start()

    def finish():
        for side in range(2):
            behind = me if side == 0 else owners - 1 - me

            @pl.when(behind >= 1)
            def _():
                copy(side, owners - 2, held.at[side, owners - 2]).wait_recv()

        right, left = held.at[0, owners - 2], held.at[1, owners - 2]
        mine = own.at[me]

        @pl.loop(0, out.shape[0] // chunk)
        def _(index):
            rows = pl.ds(pl.multiple_of(index * chunk, chunk), chunk)
            total = mine[rows, :].astype(F32)
            zero = jnp.zeros_like(total)
            total = total + jnp.where(me > 0, right[rows, :].astype(F32), zero)
            total = total + jnp.where(me < owners - 1, left[rows, :].astype(F32), zero)
            out[rows, :] = total.astype(out.dtype)

        for side in range(2):
            behind = me if side == 0 else owners - 1 - me
            for step in range(owners - 1):

                @pl.when(behind <= step)
                def _():
                    copy(side, step, held.at[side, step]).wait_send()

    return advance, finish


def line_scratch(block, owners):
    return [
        pltpu.VMEM((2, owners - 1) + block.shape[1:], block.dtype),
        pltpu.SemaphoreType.DMA((2, owners - 1)),
        pltpu.SemaphoreType.DMA((2, owners - 1)),
    ]


def line_scatter(blocks, owners, collective):
    count = len(blocks)

    def kernel(*refs):
        own, outs, scratch = refs[:count], refs[count : 2 * count], refs[2 * count :]
        me = lax.axis_index("expert")
        greet_all(me, owners, 0, 0)
        lines = []
        for i in range(count):
            held, send, recv = scratch[3 * i : 3 * i + 3]
            lines.append(scatter_line(own[i], held, outs[i], send, recv, me, owners, 32))
        for step in range(owners - 1):
            for advance, _ in lines:
                advance(step)
        for _, finish in lines:
            finish()

    return pl.pallas_call(
        kernel,
        out_shape=[jax.ShapeDtypeStruct(b.shape[1:], F32) for b in blocks],
        in_specs=[vmem_spec()] * count,
        out_specs=[vmem_spec()] * count,
        scratch_shapes=[one for b in blocks for one in line_scratch(b, owners)],
        compiler_params=kernel_params(collective),
    )(*blocks)


def column_parts(width):
    middle = width // 2 // 128 * 128
    return ((0, middle), (middle, width))


def bit_order(part, bits):
    return list(range(1, bits)) if part == 0 else list(range(bits - 1, 0, -1))


def spread(out, place, start, stop):
    return out.at[tuple(place) + (slice(None), slice(start, stop))]


def fan_out(arrays, lead, dp_index, bits, send, recv):
    def copy(slot, ref, bit, known, start, stop):
        place = lead + [
            slice(None) if one in known else bit_of(dp_index, one)
            for one in range(bits - 1, -1, -1)
        ]
        view = ref.at[tuple(place) + (slice(None), slice(start, stop))]
        return pltpu.make_async_remote_copy(
            src_ref=view,
            dst_ref=view,
            send_sem=send.at[slot],
            recv_sem=recv.at[slot],
            device_id={"dp": partner_of(dp_index, bit)},
            device_id_type=MESH,
        )

    slot = 0
    for stage in range(bits):
        going = []
        for ref in arrays:
            if stage == bits - 1:
                going.append(copy(slot, ref, 0, set(range(1, bits)), 0, ref.shape[-1]))
                slot += 1
                continue
            for part, (start, stop) in enumerate(column_parts(ref.shape[-1])):
                order = bit_order(part, bits)
                going.append(
                    copy(slot, ref, order[stage], set(order[:stage]), start, stop)
                )
                slot += 1
        for one in going:
            one.start()
        for one in going:
            one.wait()


def reduce_all(grads, blocks, owners, dp_size, collective):
    bits = dp_size.bit_length() - 1
    shapes = [(g.shape[0] // (owners * dp_size), g.shape[1]) for g in grads]
    count, extra = len(grads), len(blocks)
    pieces = [
        (i, part, start, stop)
        for i, (_, width) in enumerate(shapes)
        for part, (start, stop) in enumerate(column_parts(width))
    ]
    many = len(pieces)

    def kernel(*refs):
        take = iter(refs)
        grad_refs = [next(take) for _ in range(count)]
        block_refs = [next(take) for _ in range(extra)]
        outs = [next(take) for _ in range(count)]
        block_outs = [next(take) for _ in range(extra)]
        pairs = [next(take) for _ in range(count)]
        held = [[next(take) for _ in range(many)] for _ in range(bits - 1)]
        small = [[next(take) for _ in range(3)] for _ in range(many)]
        large = [[next(take) for _ in range(3)] for _ in range(extra)]
        fold_send, fold_recv, fan_send, fan_recv = take
        me, dp_index = lax.axis_index("expert"), lax.axis_index("dp")
        greet_all(me, owners, dp_index, bits)
        lines = [
            scatter_line(block_refs[i], large[i][0], block_outs[i], *large[i][1:], me, owners, 32)
            for i in range(extra)
        ]
        pending = [0]

        def push_lines():
            step = pending[0]
            pending[0] += 1
            for advance, finish in lines:
                if step < owners - 1:
                    advance(step)
                elif step == owners - 1:
                    finish()

        def fold(slot, bit, source, target):
            return pltpu.make_async_remote_copy(
                src_ref=source,
                dst_ref=target,
                send_sem=fold_send.at[slot],
                recv_sem=fold_recv.at[slot],
                device_id={"dp": partner_of(dp_index, bit)},
                device_id_type=MESH,
            )

        def add_all(target, source_of):
            others = list(target.shape[1:-2])

            @pl.loop(0, owners)
            def _(z):
                for flat in range(math.prod(others)):
                    place, rest = [], flat
                    for size in reversed(others):
                        place.insert(0, rest % size)
                        rest //= size
                    index = (z,) + tuple(place)
                    target[index] = (
                        target[index].astype(F32) + source_of(z, place).astype(F32)
                    ).astype(target.dtype)

        mine = bit_of(dp_index, 0)
        going = []
        for i in range(count):
            source = grad_refs[i].at[(slice(None),) * bits + (1 - mine,)]
            going.append(fold(i, 0, source, pairs[i]))
            going[-1].start()
        push_lines()
        for i in range(count):
            going[i].wait()
            add_all(pairs[i], lambda z, place: grad_refs[i][(z,) + tuple(place) + (mine,)])
        state = []
        for i, part, start, stop in pieces:
            columns = slice(start, stop)
            state.append((pairs[i], columns, sorted(range(1, bits), reverse=True)))
        for stage in range(bits - 1):
            going = []
            for index, (i, part, start, stop) in enumerate(pieces):
                ref, columns, axes = state[index]
                bit = bit_order(part, bits)[stage]
                axis = axes.index(bit)
                view = (slice(None),) * (1 + axis) + (1 - bit_of(dp_index, bit),)
                view = view + (slice(None),) * (len(axes) - axis) + (columns,)
                target = held[stage][index]
                one = fold(count + stage * many + index, bit, ref.at[view], target)
                one.start()
                going.append((one, target, ref, axis, bit, columns, axes))
            for index, (one, target, ref, axis, bit, columns, axes) in enumerate(going):
                one.wait()
                keep = bit_of(dp_index, bit)

                def source_of(z, place):
                    where = (z,) + tuple(place[:axis]) + (keep,) + tuple(place[axis:])
                    return ref[where + (slice(None), columns)]

                add_all(target, source_of)
                state[index] = (target, slice(None), [a for a in axes if a != bit])
            if stage == 0:
                push_lines()

        place = tuple(bit_of(dp_index, bit) for bit in range(bits - 1, -1, -1))
        short = []
        for index, (i, part, start, stop) in enumerate(pieces):
            rows = shapes[i][0]
            target = outs[i].at[place + (slice(None), slice(start, stop))]
            short.append(
                scatter_line(
                    state[index][0], small[index][0], target, *small[index][1:], me, owners, rows
                )
            )
        for step in range(owners - 1):
            for advance, _ in short:
                advance(step)
        for _, finish in short:
            finish()
        push_lines()
        fan_out(outs, [], dp_index, bits, fan_send, fan_recv)
        while pending[0] < owners:
            push_lines()

    scratch = []
    for rows, width in shapes:
        scratch.append(pltpu.VMEM((owners,) + (2,) * (bits - 1) + (rows, width), BF16))
    for stage in range(bits - 1):
        for i, part, start, stop in pieces:
            scratch.append(
                pltpu.VMEM(
                    (owners,) + (2,) * (bits - 2 - stage) + (shapes[i][0], stop - start), BF16
                )
            )
    for i, part, start, stop in pieces:
        block = jax.ShapeDtypeStruct((owners, shapes[i][0], stop - start), BF16)
        scratch += line_scratch(block, owners)
    for block in blocks:
        scratch += line_scratch(block, owners)
    folds = count + (bits - 1) * many
    fans = count + (bits - 1) * many
    scratch += [pltpu.SemaphoreType.DMA((folds,))] * 2 + [pltpu.SemaphoreType.DMA((fans,))] * 2
    operands = [
        g.reshape((owners,) + (2,) * bits + shape) for g, shape in zip(grads, shapes)
    ] + list(blocks)
    results = pl.pallas_call(
        kernel,
        out_shape=[jax.ShapeDtypeStruct((2,) * bits + shape, BF16) for shape in shapes]
        + [jax.ShapeDtypeStruct(b.shape[1:], F32) for b in blocks],
        in_specs=[vmem_spec()] * len(operands),
        out_specs=[vmem_spec()] * len(operands),
        scratch_shapes=scratch,
        compiler_params=kernel_params(collective),
    )(*operands)
    sums = [
        r.reshape(dp_size * rows, width) for r, (rows, width) in zip(results, shapes)
    ]
    return sums, results[count:]


def gather_rows(piece, block, owners, dp_size, collective):
    bits = dp_size.bit_length() - 1
    rows, width = piece.shape[0] // dp_size, piece.shape[1]
    shape = (owners,) + (2,) * bits + (rows, width)

    def kernel(piece_ref, block_ref, out, near, *scratch):
        line_send, line_recv, near_send, near_recv, fan_send, fan_recv, local = scratch
        me, dp_index = lax.axis_index("expert"), lax.axis_index("dp")
        greet_all(me, owners, dp_index, bits)
        place = tuple(bit_of(dp_index, bit) for bit in range(bits - 1, -1, -1))
        mine = piece_ref.at[place]

        def source_of(step, origin):
            return mine if step == 0 else out.at[(origin,) + place]

        def target_of(origin):
            return out.at[(origin,) + place]

        sides = line_sends(me, owners, source_of, target_of, line_send, line_recv, 0)
        keep = pltpu.make_async_copy(mine, out.at[(me,) + place], local)
        for step in range(owners):
            line_step(step, sides, owners)
            if step == 0:
                keep.start()
        keep.wait()

        def nearby(side):
            return pltpu.make_async_remote_copy(
                src_ref=block_ref,
                dst_ref=near.at[side],
                send_sem=near_send.at[side],
                recv_sem=near_recv.at[side],
                device_id={"expert": me + 1 - 2 * side},
                device_id_type=MESH,
            )

        ahead = (owners - 1 - me, me)
        for side in range(2):

            @pl.when(ahead[side] > 0)
            def _():
                nearby(side).start()

        fan_out([out], [slice(None)], dp_index, bits, fan_send, fan_recv)
        line_finish(sides, owners)
        for side in range(2):

            @pl.when(ahead[side] > 0)
            def _():
                nearby(side).wait_send()

            @pl.when(ahead[1 - side] > 0)
            def _():
                nearby(side).wait_recv()

    full, near = pl.pallas_call(
        kernel,
        out_shape=[
            jax.ShapeDtypeStruct(shape, BF16),
            jax.ShapeDtypeStruct((2,) + block.shape, BF16),
        ],
        in_specs=[vmem_spec()] * 2,
        out_specs=[any_spec()] * 2,
        scratch_shapes=[
            pltpu.SemaphoreType.DMA((1, 2, owners - 1)),
            pltpu.SemaphoreType.DMA((1, 2, owners - 1)),
            pltpu.SemaphoreType.DMA((2,)),
            pltpu.SemaphoreType.DMA((2,)),
            pltpu.SemaphoreType.DMA((2 * bits - 1,)),
            pltpu.SemaphoreType.DMA((2 * bits - 1,)),
            pltpu.SemaphoreType.DMA,
        ],
        compiler_params=kernel_params(collective),
    )(piece.reshape((2,) * bits + (rows, width)), block)
    return full.reshape(owners * dp_size * rows, width), near


def permute_gather(block, near, owner, owners):
    right, left = near[0], near[1]
    rightward, leftward = [right], [left]
    for step in range(1, owners - 1):
        right = lax.ppermute(right, "expert", [(z, z + 1) for z in range(step, owners - 1)])
        left = lax.ppermute(left, "expert", [(z, z - 1) for z in range(1, owners - step)])
        rightward.append(right)
        leftward.append(left)
    blocks = [block] + [
        jnp.where(owner + k < owners, leftward[k - 1], rightward[owners - k - 1])
        for k in range(1, owners)
    ]
    whole = jnp.concatenate(blocks + blocks, 0)
    return lax.dynamic_slice_in_dim(
        whole, lax.rem(owners - owner, owners) * block.shape[0], owners * block.shape[0], 0
    ).reshape((owners,) + block.shape)


def gather_slow(piece, dp_index, dp_size):
    rows = piece.shape[0] // dp_size
    part = lax.dynamic_slice_in_dim(piece, dp_index * rows, rows, 0)
    return lax.all_gather(part, ("expert", "dp"), axis=0, tiled=True)


def per_device(
    tokens,
    seq_lengths,
    routes,
    norm_attn,
    query_key_value_weight,
    w_out,
    norm_moe,
    router,
    expert_in,
    expert_out,
    cotangent,
):
    owners = lax.axis_size("expert")
    dp_size = lax.axis_size("dp")
    owner = lax.axis_index("expert")
    dp_index = lax.axis_index("dp")
    _, length, width = tokens.shape
    query_groups = QUERY_HEADS // KEY_VALUE_HEADS
    local_experts = expert_in.shape[0]
    experts = local_experts * owners
    capacity = length * TOPK // experts
    scale_factor = HEAD_SIZE ** (-0.5)
    query_width = QUERY_HEADS * HEAD_SIZE
    key_width = KEY_VALUE_HEADS * HEAD_SIZE
    qkv_width = query_width + 2 * key_width

    small = jnp.concatenate(
        [
            router,
            norm_attn[:, None],
            norm_moe[:, None],
            jnp.zeros((router.shape[0], AUX - experts - 2), BF16),
        ],
        1,
    )
    qkv_packed, near = gather_rows(
        jnp.concatenate([query_key_value_weight, small], 1), cotangent[0], owners, dp_size, 1
    )
    out_full = gather_slow(w_out, dp_index, dp_size)
    upstream_all = permute_gather(cotangent[0], near, owner, owners)
    small_full = qkv_packed[:, qkv_width:].astype(F32)
    router_wide = small_full[:, :experts]
    gain_first = small_full[:, experts]
    gain_second = small_full[:, experts + 1]

    sequence_live = seq_lengths[0]
    position = jnp.arange(length)
    live = position < sequence_live
    live_rows = live[:, None].astype(F32)
    inputs = tokens[0].astype(F32)
    normed_first, factor_first = norm_apply(inputs, gain_first)
    normed_low = normed_first.astype(BF16)
    projected_rows = dot("td,df->tf", normed_low, qkv_packed)
    cosine, sine_table = tables(length, HEAD_SIZE)
    cos_four = cosine[:, None, None, :]
    sin_four = sine_table[:, None, None, :]
    cos_three = cosine[:, None, :]
    sin_three = sine_table[:, None, :]
    query_rows = rotate(
        projected_rows[:, :query_width].reshape(length, KEY_VALUE_HEADS, query_groups, HEAD_SIZE),
        cos_four,
        sin_four,
    ).astype(BF16)
    key_rows_all = rotate(
        projected_rows[:, query_width : query_width + key_width].reshape(
            length, KEY_VALUE_HEADS, HEAD_SIZE
        ),
        cos_three,
        sin_three,
    ).astype(BF16)
    value_rows = (
        projected_rows[:, query_width + key_width : qkv_width]
        .reshape(length, KEY_VALUE_HEADS, HEAD_SIZE)
        .astype(BF16)
    )
    attended, log_total = attend_forward(
        query_rows, key_rows_all, value_rows, sequence_live, scale_factor
    )
    hidden_sum = inputs + dot("ti,id->td", attended, out_full)
    normed_second, factor_second = norm_apply(hidden_sum, gain_second)
    second_low = normed_second.astype(BF16)

    chosen = jnp.any(routes[0][:, :, None] == jnp.arange(experts)[None, None, :], 1)
    pairs = chosen & live[:, None]
    earlier = (position[:, None] > position[None, :]).astype(BF16)
    ranking = dot("tu,ue->te", earlier, pairs.astype(BF16))
    kept = pairs & (ranking < capacity)
    logits = jnp.dot(second_low.astype(F32), router_wide, precision=PRECISE)
    topmost = jnp.max(jnp.where(chosen, logits, -jnp.inf), -1, keepdims=True)
    exponent = jnp.where(chosen, jnp.exp(jnp.where(chosen, logits - topmost, 0.0)), 0.0)
    gating = exponent / jnp.sum(exponent, -1, keepdims=True)
    kept_weight = jnp.where(kept, gating, 0.0)
    slot_of = jnp.where(kept, ranking, -1.0).astype(BF16)
    weight_high, weight_low = split_two(kept_weight)
    extra = jnp.concatenate(
        [slot_of, weight_high, weight_low, jnp.zeros((length, AUX - 3 * experts), BF16)], 1
    )
    rows_all, extra_all = line_gather([second_low, extra], owners, 2)
    extra_all = extra_all.astype(F32)

    def own(column):
        return lax.dynamic_slice_in_dim(
            extra_all, column * experts + owner * local_experts, local_experts, 2
        )

    slots = own(0)
    weights_all = own(1) + own(2)
    hits = slots.transpose(0, 2, 1)[:, :, None, :] == jnp.arange(capacity, dtype=F32)[:, None]
    picks = hits.astype(BF16)
    slot_weight = jnp.sum(
        jnp.where(hits, weights_all.transpose(0, 2, 1)[:, :, None, :], 0.0), -1
    )
    inner_full = lax.all_gather(expert_in, "dp", axis=1, tiled=True)
    down_full = lax.all_gather(expert_out, "dp", axis=1, tiled=True)
    hidden_width = down_full.shape[1]

    rows_in = dot("sect,std->escd", picks, rows_all).astype(BF16)
    grad_in = dot("sect,std->escd", picks, upstream_all).astype(BF16)
    gate_up = dot("escd,edf->escf", rows_in, inner_full)
    gate_part = gate_up[..., :hidden_width]
    up_part = gate_up[..., hidden_width:]
    sigmoid_part = jax.nn.sigmoid(gate_part)
    activated = gate_part * sigmoid_part
    hidden = activated * up_part
    weight_column = slot_weight.transpose(1, 0, 2)[..., None]
    hidden_weighted = (hidden * weight_column).astype(BF16)
    hidden_grad = dot("escd,ehd->esch", grad_in, down_full)
    gate_grad_slot = jnp.sum(hidden.astype(BF16).astype(F32) * hidden_grad, -1)
    hidden_grad = hidden_grad * weight_column
    gate_part_grad = hidden_grad * up_part * sigmoid_part * (1.0 + gate_part * (1.0 - sigmoid_part))
    up_grad = hidden_grad * activated
    gate_up_grad = jnp.concatenate([gate_part_grad, up_grad], -1).astype(BF16)
    row_grad = dot("escf,edf->escd", gate_up_grad, inner_full).astype(BF16)
    back = dot("sect,escd->std", picks, row_grad).astype(BF16)
    gate_grad_own = jnp.sum(
        jnp.where(hits, gate_grad_slot.transpose(1, 0, 2)[..., None], 0.0), 2
    ).transpose(0, 2, 1)
    gate_wide = jnp.zeros((owners, length, experts), F32)
    gate_wide = lax.dynamic_update_slice_in_dim(gate_wide, gate_grad_own, owner * local_experts, 2)
    gate_packed = jnp.concatenate(
        list(split_two(gate_wide)) + [jnp.zeros((owners, length, AUX - 2 * experts), BF16)], 2
    )
    inner_weight_grad = dot("escd,escf->edf", rows_in, gate_up_grad).astype(BF16)
    down_weight_grad = dot("esch,escd->ehd", hidden_weighted, grad_in).astype(BF16)
    back, inner_weight_grad, down_weight_grad = lax.optimization_barrier(
        (back, inner_weight_grad, down_weight_grad)
    )
    inner_sum = lax.psum_scatter(
        inner_weight_grad, "dp", scatter_dimension=1, tiled=True
    ).astype(F32)
    down_sum = lax.psum_scatter(
        down_weight_grad, "dp", scatter_dimension=1, tiled=True
    ).astype(F32)
    back_sum, gate_sum = line_scatter([back, gate_packed], owners, 3)
    back_sum, hidden_late = lax.optimization_barrier((back_sum, hidden_weighted))
    expert_rows = dot("esch,ehd->escd", hidden_late, down_full).astype(BF16)
    mixed = dot("sect,escd->std", picks, expert_rows).astype(BF16)

    upstream = cotangent[0].astype(F32) * live_rows
    gate_grad = gate_sum[:, :experts] + gate_sum[:, experts : 2 * experts]
    logit_grad = gating * (gate_grad - jnp.sum(gating * gate_grad, -1, keepdims=True))
    second_grad = back_sum + jnp.dot(
        logit_grad, router_wide.T, precision=PRECISE
    )
    router_grad = jnp.dot(second_low.astype(F32).T, logit_grad, precision=PRECISE)
    hidden_back, gain_two_grad = norm_back(hidden_sum, factor_second, gain_second, second_grad)
    total_grad = upstream + hidden_back
    total_low = total_grad.astype(BF16)
    out_weight_grad = dot("ti,td->id", attended, total_low)
    attended_grad = dot("td,id->ti", total_low, out_full).astype(BF16)
    query_grad, key_grad, value_grad = attend_backward(
        query_rows, key_rows_all, value_rows, sequence_live, log_total, attended_grad, scale_factor
    )
    query_grad = rotate(query_grad, cos_four, -sin_four)
    key_grad = rotate(key_grad, cos_three, -sin_three)
    projected_grad = jnp.concatenate(
        [
            query_grad.reshape(length, -1),
            key_grad.reshape(length, -1),
            value_grad.reshape(length, -1),
            jnp.zeros((length, AUX), F32),
        ],
        -1,
    ).astype(BF16)
    qkv_weight_grad = dot("td,tf->df", normed_low, projected_grad)
    first_grad = dot("tf,df->td", projected_grad, qkv_packed)
    input_back, gain_one_grad = norm_back(inputs, factor_first, gain_first, first_grad)
    input_grad = (total_grad + input_back).astype(BF16)
    small_grad = jnp.concatenate(
        [
            router_grad,
            gain_one_grad[:, None],
            gain_two_grad[:, None],
            jnp.zeros((width, AUX - experts - 2), F32),
        ],
        1,
    )
    packed_grad = lax.dynamic_update_slice(
        qkv_weight_grad.astype(BF16), small_grad.astype(BF16), (0, qkv_width)
    )
    grads = [packed_grad, out_weight_grad.astype(BF16)]
    if owners > 4:
        (packed_sum, out_sum), _ = reduce_all(grads, [], owners, dp_size, 4)
        (mixture,) = line_scatter([mixed], owners, 5)
    else:
        (packed_sum, out_sum), (mixture,) = reduce_all(grads, [mixed], owners, dp_size, 4)
    packed_sum = packed_sum.astype(F32)
    output = (live_rows * (hidden_sum + mixture)).astype(BF16)
    return (
        output[None],
        input_grad[None],
        packed_sum[:, qkv_width + experts],
        packed_sum[:, :qkv_width],
        out_sum.astype(F32),
        packed_sum[:, qkv_width + experts + 1],
        packed_sum[:, qkv_width : qkv_width + experts],
        inner_sum,
        down_sum,
    )


def solution(mesh):
    return jax.shard_map(
        per_device,
        mesh=mesh,
        in_specs=(
            P(("dp", "expert"), None, None),
            P(("dp", "expert")),
            P(("dp", "expert"), None, None),
            P("expert"),
            P("expert", None),
            P("expert", None),
            P("expert"),
            P("expert", None),
            P("expert", "dp", None),
            P("expert", "dp", None),
            P(("dp", "expert"), None, None),
        ),
        out_specs=(
            P(("dp", "expert"), None, None),
            P(("dp", "expert"), None, None),
            P("expert"),
            P("expert", None),
            P("expert", None),
            P("expert"),
            P("expert", None),
            P("expert", "dp", None),
            P("expert", "dp", None),
        ),
        check_vma=False,
    )
```

time: 2130 us -> 976 us (0.46)
  waiting for transfers between devices: 1260 us -> 30.6 us
  Pallas kernels: 0 us -> 473 us
  local copies, waits for them, and re-layouts: 353 us -> 51.2 us
  blocking collectives: 81.5 us -> 0 us
    all_to_all x4 -> x0, waiting for transfers between devices: 967 us -> none  [the longest x1 262 us: per_device(): lax.all_to_all(send_rows.reshape(owners, local_experts * capacity, model_...]
    pallas_call x0 -> x4, Pallas kernels: none -> 473 us  [the longest x1 160 us: reduce_all(): pl.pallas_call(kernel, out_shape=[jax.ShapeDtypeStruct((2,) * bits + shap...]
    gather x10 -> x0, local copies, waits for them, and re-layouts: 171 us -> none  [the longest x2 41.9 us: per_device(): upstream[slot_token]]
    reduce_scatter x4 -> x2, waiting for transfers between devices: 164 us -> 0.01 us  [the longest x1 0.01 us: per_device(): lax.psum_scatter(down_weight_grad, 'dp', scatter_dimension=1, tiled=True)]
    psum x1 -> x0, waiting for transfers between devices: 68.7 us -> none  [per_device(): lax.psum(shards[0].astype(jnp.bfloat16), 'dp').astype(jnp.float32)]
    reshape x6 -> x0, local copies, waits for them, and re-layouts: 67.6 us -> none  [the longest x1 15.1 us: per_device(): row_back = lax.all_to_all(row_grad.reshape(owners, local_experts * capaci...]
    all_gather x4 -> x3, waiting for transfers between devices: 56.4 us -> 0.01 us  [the longest x1 0.01 us: gather_slow(): return lax.all_gather(part, ('expert', 'dp'), axis=0, tiled=True)]
    scatter x3 -> x0, local copies, waits for them, and re-layouts: 48.9 us -> none  [the longest x1 17.7 us: per_device(): jnp.zeros((slot_count + 1,), jnp.bool_).at[slot_index].set(kept_pairs)]
  transfers between devices with their start and end apart: 14 -> 9, of which waited for: 10 -> 1; matrix products, arithmetic and copies ran while one was open for 31% -> 33% of each run, Pallas kernels for 0% -> 49%
where the time goes in v1:
time: 976 us; the launch traced here: 968 us
  Pallas kernels  473 us (48%)
  matrix products  293 us (30%)
  other arithmetic  97.5 us (10%)
  local copies, waits for them, and re-layouts  51.2 us (5%)
  waiting for transfers between devices  30.6 us (3%)
  between operations  16 us (2%)
    dot_general x22, matrix products, dot(): return jnp.einsum(spec, a, b, preferred_element_type=F32)  285 us
    pallas_call x1, Pallas kernels, reduce_all(): pl.pallas_call(kernel, out_shape=[jax.ShapeDtypeStruct((2,) * bits + shap...  160 us
    pallas_call x1, Pallas kernels, line_scatter(): pl.pallas_call(kernel, out_shape=[jax.ShapeDtypeStruct(b.shape[1:], F32)...  116 us
    pallas_call x1, Pallas kernels, line_gather(): pl.pallas_call(kernel, out_shape=[jax.ShapeDtypeStruct((owners,) + b.shap...  114 us
    pallas_call x1, Pallas kernels, gather_rows(): pl.pallas_call(kernel, out_shape=[jax.ShapeDtypeStruct(shape, BF16), jax....  83.7 us
    ppermute x2, waiting for transfers between devices, permute_gather(): lax.ppermute(left, 'expert', [(z, z - 1) for z in range(1, owners - step)])  29.3 us
    convert_element_type x1, other arithmetic, attend_backward(): score_grad = (weights * (weight_grad - jnp.sum(weights * weight_grad, -1,...  23.2 us
  transfers between devices with their start and end apart: 9, of which 1 were waited for; matrix products, arithmetic and copies ran while one was open for 33% of the time, Pallas kernels for 49%

profile of v1, /device:TPU:0, one launch (start us, length us, event | category | flops | bytes accessed | tf_op | source)
XLA Modules:
  0.0 967.7 jit_solution(15260172872668858166)
XLA Ops:
  12.7 4.5 concatenate.53.piece_ref
  17.2 83.7 %shard_map.178 = (bf16[4,2,2,2,48,2688]{5,4,3,2,1,0:T(8,128)(2,1)}, bf16[2,512,1536]{2,1,0:T(8,128)(2,1)}) custom-call(bf16[2,2,2,48,2688]{4,3,2,1,0:T(8,128)(2,1)} %concatenate.53.piece_ref, bf16[512,1536]{1,0:T(8,128)(2,1)} %bitcast.216), custom_call_target="tpu_custom_call" | custom-call | tf_op jit(solution)/shard_map/pallas_call | solution.py:604
  110.3 7.6 fusion.69
  132.8 11.7 %fusion.22 = (f32[8,3,512]{2,1,0:T(4,128)S(1)}, f32[8,512,512,3]{2,1,3,0:T(8,128)}) fusion(pred[512,512]{0,1:T(8,128)(4,1)S(1)} %fusion.85, bf16[512,8,3,32]{0,3,2,1:T(8,128)(2,1)S(1)} %get-tuple-element.59, bf16[512,8,3,32]{0,3,2,1:T(8,128)(2,1)S(1)} %get-tuple-element.58, bf16[512,8,32]{0,2,1:T(8,128)(2,1)} %get-tuple-element.65, ...), kind=kOutput, calls=%fused_computation.34 | convolution fusion | flops 828362752 | bytes 27574272 | tf_op jit(solution)/shard_map/qgrh,kgh->grqk/dot_general | solution.py:59
  144.5 11.3 %fusion.3 = f32[8,3,512]{2,1,0:T(4,128)S(1)} fusion(f32[8,3,512]{2,1,0:T(4,128)S(1)} %get-tuple-element.71, f32[8,512,512,3]{2,1,3,0:T(8,128)} %get-tuple-element.72, pred[512,512]{0,1:T(8,128)(4,1)S(1)} %fusion.85), kind=kLoop, calls=%fused_computation.10 | loop fusion | flops 25153536 | bytes 25526272 | tf_op jit(solution)/shard_map/reduce_sum | solution.py:74
  158.0 13.2 %fusion.66 = bf16[8,64,3,512]{3,1,2,0:T(8,128)(2,1)} fusion(bf16[512,8,64,1]{0,2,3,1:T(8,128)(2,1)S(1)} %bitcast.224, f32[8,3,512]{2,1,0:T(4,128)S(1)} %fusion.3, f32[8,3,512]{2,1,0:T(4,128)S(1)} %get-tuple-element.71, f32[8,512,512,3]{2,1,3,0:T(8,128)} %get-tuple-element.72, pred[512,512]{0,1:T(8,128)(4,1)S(1)} %fusion.85), kind=kOutput, calls=%fused_computation.89 | convolution fusion | flops 837550080 | bytes 27623424 | tf_op jit(solution)/shard_map/grqk,kgh->qgrh/dot_general | solution.py:59
  180.9 29.3 %collective-permute-done.3 = bf16[512,1536]{1,0:T(8,128)(2,1)} collective-permute-done((bf16[512,1536]{1,0:T(8,128)(2,1)}, bf16[512,1536]{1,0:T(8,128)(2,1)}, u32[]{:S(2)}, u32[]{:S(2)}) %collective-permute-start.3) | collective-permute-done | bytes 1572896 | tf_op jit(solution)/shard_map/ppermute | solution.py:631
  221.8 6.0 constant_dynamic-slice_fusion
  227.9 5.3 multiply_reduce_fusion.3
  238.5 113.5 %shard_map.179 = (bf16[4,512,1536]{2,1,0:T(8,128)(2,1)}, bf16[4,512,128]{2,1,0:T(8,128)(2,1)}) custom-call(bf16[512,1536]{1,0:T(8,128)(2,1)} %copy-done.7, bf16[512,128]{1,0:T(8,128)(2,1)} %maximum_maximum_fusion.2.refs_1_), custom_call_target="tpu_custom_call" | custom-call | tf_op jit(solution)/shard_map/pallas_call | solution.py:221
  354.7 12.8 %convert_bitcast_fusion.1 = bf16[5,4,204,1536]{3,2,0,1:T(8,128)(2,1)} fusion(bf16[4,512,1536,1]{2,1,3,0:T(8,128)(2,1)} %bitcast.220, f32[4,5,512]{2,1,0:T(8,128)S(1)} %copy.152), kind=kOutput, calls=%fused_computation.23 | convolution fusion | flops 6425640960 | bytes 18866176 | tf_op jit(solution)/shard_map/sect,std->escd/dot_general | solution.py:59
  367.5 12.4 %convert_bitcast_fusion = bf16[5,4,204,1536]{3,2,0,1:T(8,128)(2,1)} fusion(bf16[4,512,1536]{2,1,0:T(8,128)(2,1)} %get-tuple-element.26, f32[4,5,512]{2,1,0:T(8,128)S(1)} %copy.152), kind=kOutput, calls=%fused_computation.22 | convolution fusion | flops 6425640960 | bytes 18866176 | tf_op jit(solution)/shard_map/sect,std->escd/dot_general | solution.py:59
  379.9 24.2 %fusion.5 = f32[5,4,204,1024]{3,2,1,0:T(8,128)} fusion(bf16[5,1536,1024]{2,1,0:T(8,128)(2,1)} %all-gather.8.cloned.1.call-done, bf16[5,4,204,1536]{3,2,0,1:T(8,128)(2,1)} %convert_bitcast_fusion), kind=kOutput, calls=%fused_computation.12 | convolution fusion | flops 12834570240 | bytes 44974080 | tf_op jit(solution)/shard_map/escd,edf->escf/dot_general | solution.py:59
  404.1 17.1 %multiply_reduce_fusion = (f32[5,4,204]{2,1,0:T(4,128)S(1)}, f32[5,4,204,512]{3,2,1,0:T(8,128)S(1)}) fusion(f32[5,4,204,1024]{3,2,1,0:T(8,128)} %fusion.5, bf16[5,512,1536]{2,1,0:T(8,128)(2,1)} %all-gather.6.cloned.1.call-done, bf16[5,4,204,1536]{3,2,0,1:T(8,128)(2,1)} %convert_bitcast_fusion.1), kind=kOutput, calls=%fused_computation.37 | convolution fusion | flops 6436081664 | bytes 45481920 | tf_op jit(solution)/shard_map/escd,ehd->esch/dot_general | solution.py:59
  423.7 12.3 %multiply_convert_fusion.2 = (bf16[5,4,204,512]{3,2,1,0:T(8,128)(2,1)}, bf16[5,4,204,512]{3,2,1,0:T(8,128)(2,1)}, bf16[5,4,204,512]{3,2,1,0:T(8,128)(2,1)}) fusion(f32[5,4,204,1024]{3,2,1,0:T(8,128)} %fusion.5, f32[5,4,204,512]{3,2,1,0:T(8,128)S(1)} %get-tuple-element.78, f32[5,4,204]{2,1,0:T(4,128)S(1)} %copy.155), kind=kLoop, calls=%fused_computation.40 | loop fusion | flops 35512320 | bytes 37617600 | tf_op jit(solution)/shard_map/convert.21
  436.0 15.8 %bitcast_convert_fusion.1 = bf16[5,512,1536]{2,1,0:T(8,128)(2,1)} fusion(bf16[5,4,204,512]{3,2,1,0:T(8,128)(2,1)} %get-tuple-element.31, bf16[5,4,204,1536]{3,2,0,1:T(8,128)(2,1)} %convert_bitcast_fusion.1), kind=kOutput, calls=%fused_computation.14 | convolution fusion | flops 6421217280 | bytes 24576000 | tf_op jit(solution)/shard_map/esch,escd->ehd/dot_general | solution.py:59
  451.8 24.4 %bitcast_convert_fusion = bf16[5,1536,1024]{2,1,0:T(8,128)(2,1)} fusion(bf16[5,4,204,1536]{3,2,0,1:T(8,128)(2,1)} %convert_bitcast_fusion, bf16[5,4,204,512]{3,2,1,0:T(8,128)(2,1)} %get-tuple-element.54, bf16[5,4,204,512]{3,2,1,0:T(8,128)(2,1)} %get-tuple-element.53), kind=kOutput, calls=%fused_computation | convolution fusion | flops 12859146240 | bytes 36618240 | tf_op jit(solution)/shard_map/escd,escf->edf/dot_general | solution.py:59
  476.2 24.7 %fusion.7 = bf16[5,4,204,1536]{3,2,0,1:T(8,128)(2,1)} fusion(bf16[5,1536,1024]{2,1,0:T(8,128)(2,1)} %all-gather.8.cloned.1.call-done, bf16[5,4,204,512]{3,2,1,0:T(8,128)(2,1)} %get-tuple-element.54, bf16[5,4,204,512]{3,2,1,0:T(8,128)(2,1)} %get-tuple-element.53), kind=kOutput, calls=%fused_computation.15 | convolution fusion | flops 12851281920 | bytes 36618240 | tf_op jit(solution)/shard_map/escf,edf->escd/dot_general | solution.py:59
  501.0 15.2 %bitcast_convert_fusion.3.refs_0_ = bf16[4,512,1536]{2,1,0:T(8,128)(2,1)} fusion(bf16[5,4,204,1536]{3,2,0,1:T(8,128)(2,1)} %fusion.7, f32[4,5,512]{2,1,0:T(8,128)S(1)} %copy.152), kind=kOutput, calls=%fused_computation.26 | convolution fusion | flops 6422519808 | bytes 18866176 | tf_op jit(solution)/shard_map/sect,escd->std/dot_general | solution.py:59
  517.6 4.5 dynamic_update_slice.6
  523.3 115.6 %shard_map.180 = (f32[512,1536]{1,0:T(8,128)}, f32[512,128]{1,0:T(8,128)}) custom-call(bf16[4,512,1536]{2,1,0:T(8,128)(2,1)} %bitcast_convert_fusion.3.refs_0_, bf16[4,512,128]{2,1,0:T(8,128)(2,1)} %maximum_maximum_fusion.1.refs_1_), custom_call_target="tpu_custom_call" | custom-call | tf_op jit(solution)/shard_map/pallas_call | solution.py:331
  641.6 5.7 multiply_reduce_fusion.1
  655.5 21.6 %fusion = (f32[8,3,512]{2,1,0:T(4,128)S(1)}, f32[8,512,512,3]{2,1,3,0:T(8,128)}) fusion(f32[8,3,512]{2,1,0:T(4,128)S(1)} %log_add_fusion, f32[8,512,512,3]{2,1,3,0:T(8,128)} %get-tuple-element.72, pred[512,512]{0,1:T(8,128)(4,1)S(1)} %copy-done.17, bf16[512,8,64,1]{0,2,3,1:T(8,128)(2,1)S(1)} %bitcast.225, bf16[512,8,3,64]{0,3,2,1:T(8,128)(2,1)S(1)} %bitcast.218), kind=kOutput, calls=%fused_computation.3 | convolution fusion | flops 836751360 | bytes 52789248 | tf_op jit(solution)/shard_map/qgrh,kgh->grqk/dot_general | solution.py:59
  677.1 23.2 %fusion.2 = bf16[8,3,512,512]{2,3,1,0:T(8,128)(2,1)} fusion(f32[8,512,512,3]{2,1,3,0:T(8,128)} %get-tuple-element.81, f32[8,3,512]{2,1,0:T(4,128)S(1)} %get-tuple-element.80, f32[8,3,512]{2,1,0:T(4,128)S(1)} %log_add_fusion, f32[8,512,512,3]{2,1,3,0:T(8,128)} %get-tuple-element.72, pred[512,512]{0,1:T(8,128)(4,1)S(1)} %copy-done.17), kind=kLoop, calls=%fused_computation.5 | loop fusion | flops 37748736 | bytes 63275008 | tf_op jit(solution)/shard_map/convert_element_type | solution.py:90
  700.4 8.6 fusion.81
  709.3 7.0 multiply_bitcast_fusion
  717.1 12.1 %fusion.82 = bf16[8,64,512]{2,1,0:T(8,128)(2,1)S(1)} fusion(bf16[512,8,3,64]{0,3,2,1:T(8,128)(2,1)S(1)} %bitcast.219, f32[8,3,512]{2,1,0:T(4,128)S(1)} %log_add_fusion, f32[8,512,512,3]{2,1,3,0:T(8,128)} %get-tuple-element.72, pred[512,512]{0,1:T(8,128)(4,1)S(1)} %copy-done.17), kind=kOutput, calls=%fused_computation.113 | convolution fusion | flops 830734336 | bytes 27574272 | tf_op jit(solution)/shard_map/grqk,qgrh->kgh/dot_general | solution.py:59
  729.2 10.8 %fusion.58 = (f32[512]{0:T(512)S(1)}, bf16[1536]{0:T(1024)(128)(2,1)S(1)}, f32[512,1536]{1,0:T(8,128)}) fusion(bf16[1,512,1536]{2,1,0:T(8,128)(2,1)S(1)} %copy-done.14, f32[1536]{0:T(1024)S(1)} %copy-done.45, f32[512]{0:T(512)S(1)} %copy-done.48, bf16[1536,2688]{1,0:T(8,128)(2,1)} %bitcast.236, bf16[512,512]{0,1:T(8,128)(2,1)S(1)} %bitcast.244, ...), kind=kOutput, calls=%fused_computation.70 | convolution fusion | flops 4244371456 | bytes 15616256 | tf_op jit(solution)/shard_map/tf,df->td/dot_general | solution.py:59
  741.7 10.9 %convolution_convert_fusion = bf16[1536,2688]{1,0:T(8,128)(2,1)} fusion(bf16[1,512,1536]{2,1,0:T(8,128)(2,1)S(1)} %copy-done.15, f32[1536]{0:T(1024)S(1)} %copy-done.45, f32[512]{0:T(512)S(1)} %copy-done.48, bf16[512,512]{0,1:T(8,128)(2,1)} %bitcast.245, bf16[512,512]{0,1:T(8,128)(2,1)} %bitcast.230, bf16[512,1536]{0,1:T(8,128)(2,1)} %bitcast.228, ...), kind=kOutput, calls=%fused_computation.29 | convolution fusion | flops 4246142976 | bytes 12465408 | tf_op jit(solution)/shard_map/td,tf->df/dot_general | solution.py:59
  758.0 20.9 %bitcast_convert_fusion.2.refs_2_ = bf16[4,512,1536]{2,1,0:T(8,128)(2,1)} fusion(f32[4,5,512]{2,1,0:T(8,128)S(1)} %copy.152, bf16[5,512,1536]{2,1,0:T(8,128)(2,1)} %all-gather.6.cloned.1.call-done, bf16[5,4,204,512]{3,2,1,0:T(8,128)(2,1)} %get-tuple-element.31), kind=kOutput, calls=%fused_computation.25 | convolution fusion | flops 12846071808 | bytes 18374656 | tf_op jit(solution)/shard_map/sect,escd->std/dot_general | solution.py:59
  778.9 159.9 %shard_map.181 = (bf16[2,2,2,48,2688]{4,3,2,1,0:T(8,128)(2,1)}, bf16[2,2,2,48,1536]{4,3,2,1,0:T(8,128)(2,1)}, f32[512,1536]{1,0:T(8,128)}) custom-call(bf16[4,2,2,2,48,2688]{5,4,3,2,1,0:T(8,128)(2,1)} %bitcast.56.refs_0_, bf16[4,2,2,2,48,1536]{5,4,3,2,1,0:T(8,128)(2,1)} %bitcast.221, bf16[4,512,1536]{2,1,0:T(8,128)(2,1)} %bitcast_convert_fusion.2.refs_2_), custom_call_target="tpu_custom_call" | custom-call | tf_op jit(solution)/shard_map/pallas_call | solution.py:534
  948.5 5.6 fusion.67
  (219 shorter events, 100.1 us)
Async XLA Ops:
  7.2 220.7 %all-gather.4.cloned.1.call-start = ((), (), s32[]{:S(2)}) async-start(), calls=%async_computation.2 | async-start | bytes 4866048 | tf_op jit(solution)/shard_map/all_gather | solution.py:647
  9.1 370.7 %all-gather.8.cloned.1.call-start = ((), (), s32[]{:S(2)}) async-start(), calls=%async_computation.4 | async-start | bytes 17694720 | tf_op jit(solution)/shard_map/all_gather | solution.py:763
  9.9 394.2 %all-gather.6.cloned.1.call-start = ((), (), s32[]{:S(2)}) async-start(), calls=%async_computation.3 | async-start | bytes 8847360 | tf_op jit(solution)/shard_map/all_gather | solution.py:764
  105.3 50.5 %collective-permute-start = (bf16[512,1536]{1,0:T(8,128)(2,1)}, bf16[512,1536]{1,0:T(8,128)(2,1)}, u32[]{:S(2)}, u32[]{:S(2)}) collective-permute-start(bf16[512,1536]{1,0:T(8,128)(2,1)} %get-tuple-element.61), channel_id=1, source_target_pairs={{1,2},{2,3},{5,6},{6,7},{9,10},{10,11},{13,14},{14,15},{17,18},{18... | collective-permute-start | bytes 4718600 | tf_op jit(solution)/shard_map/ppermute | solution.py:630
  107.1 64.1 %collective-permute-start.2 = (bf16[512,1536]{1,0:T(8,128)(2,1)}, bf16[512,1536]{1,0:T(8,128)(2,1)}, u32[]{:S(2)}, u32[]{:S(2)}) collective-permute-start(bf16[512,1536]{1,0:T(8,128)(2,1)} %get-tuple-element.60), channel_id=1, source_target_pairs={{1,0},{2,1},{5,4},{6,5},{9,8},{10,9},{13,12},{14,13},{17,16},{18,1... | collective-permute-start | bytes 4718600 | tf_op jit(solution)/shard_map/ppermute | solution.py:631
  108.5 845.6 %reduce-scatter.5.cloned.1.call-start = ((), (), s32[]{:S(2)}) async-start(), calls=%async_computation.6 | async-start | bytes 8847360 | tf_op jit(solution)/shard_map/reduce_scatter | solution.py:801
  109.9 123.3 %copy-start.40 = (f32[1536]{0:T(1024)}, f32[1536]{0:T(1024)S(1)}, u32[]{:S(2)}) copy-start(f32[1536]{0:T(1024)S(1)} %get-tuple-element.43) | copy-start | bytes 18436
  129.5 15.0 %copy-start.21 = (bf16[512,8,3,32]{0,3,2,1:T(8,128)(2,1)}, bf16[512,8,3,32]{0,3,2,1:T(8,128)(2,1)S(1)}, u32[]{:S(2)}) copy-start(bf16[512,8,3,32]{0,3,2,1:T(8,128)(2,1)S(1)} %get-tuple-element.58) | copy-start | bytes 2359300
  129.5 15.0 %copy-start.23 = (bf16[512,8,3,32]{0,3,2,1:T(8,128)(2,1)}, bf16[512,8,3,32]{0,3,2,1:T(8,128)(2,1)S(1)}, u32[]{:S(2)}) copy-start(bf16[512,8,3,32]{0,3,2,1:T(8,128)(2,1)S(1)} %get-tuple-element.59) | copy-start | bytes 2359300
  131.4 26.5 %copy-start.16 = (pred[512,512]{0,1:T(8,128)(4,1)}, pred[512,512]{0,1:T(8,128)(4,1)S(1)}, u32[]{:S(2)}) copy-start(pred[512,512]{0,1:T(8,128)(4,1)S(1)} %fusion.85) | copy-start | bytes 786436
  132.8 25.2 %copy-start.26 = (bf16[512,512]{0,1:T(8,128)(2,1)}, bf16[512,512]{0,1:T(8,128)(2,1)S(1)}, u32[]{:S(2)}) copy-start(bf16[512,512]{0,1:T(8,128)(2,1)S(1)} %copy.142) | copy-start | bytes 1572868
  144.5 13.4 %copy-start.36 = (f32[8,3,512]{2,1,0:T(4,128)}, f32[8,3,512]{2,1,0:T(4,128)S(1)}, u32[]{:S(2)}) copy-start(f32[8,3,512]{2,1,0:T(4,128)S(1)} %get-tuple-element.71) | copy-start | bytes 147460
  155.8 15.4 %copy-start.38 = (f32[8,3,512]{2,1,0:T(4,128)}, f32[8,3,512]{2,1,0:T(4,128)S(1)}, u32[]{:S(2)}) copy-start(f32[8,3,512]{2,1,0:T(4,128)S(1)} %fusion.3) | copy-start | bytes 147460
  155.9 18.7 %collective-permute-start.1 = (bf16[512,1536]{1,0:T(8,128)(2,1)}, bf16[512,1536]{1,0:T(8,128)(2,1)}, u32[]{:S(2)}, u32[]{:S(2)}) collective-permute-start(bf16[512,1536]{1,0:T(8,128)(2,1)} %collective-permute-done), channel_id=1, source_target_pairs={{2,3},{6,7},{10,11},{14,15},{18,19},{22,23},{26,27},{30,31}} | collective-permute-start | bytes 4718600 | tf_op jit(solution)/shard_map/ppermute | solution.py:630
  158.0 14.6 %copy-start.5 = (bf16[1,512,1536]{2,1,0:T(8,128)(2,1)S(1)}, bf16[1,512,1536]{2,1,0:T(8,128)(2,1)}, u32[]{:S(2)}) copy-start(bf16[1,512,1536]{2,1,0:T(8,128)(2,1)} %param.21) | copy-start | bytes 4718596
  158.0 15.8 %copy-start.46 = (s32[1,512,8]{1,2,0:T(8,128)S(1)}, s32[1,512,8]{1,2,0:T(8,128)}, u32[]{:S(2)}) copy-start(s32[1,512,8]{1,2,0:T(8,128)} %param.13) | copy-start | bytes 49156
  171.2 39.0 %collective-permute-start.3 = (bf16[512,1536]{1,0:T(8,128)(2,1)}, bf16[512,1536]{1,0:T(8,128)(2,1)}, u32[]{:S(2)}, u32[]{:S(2)}) collective-permute-start(bf16[512,1536]{1,0:T(8,128)(2,1)} %collective-permute-done.2), channel_id=1, source_target_pairs={{1,0},{5,4},{9,8},{13,12},{17,16},{21,20},{25,24},{29,28}} | collective-permute-start | bytes 4718600 | tf_op jit(solution)/shard_map/ppermute | solution.py:631
  174.6 35.6 %copy-start.4 = (bf16[2,512,1536]{2,1,0:T(8,128)(2,1)S(1)}, bf16[2,512,1536]{2,1,0:T(8,128)(2,1)}, u32[]{:S(2)}) copy-start(bf16[2,512,1536]{2,1,0:T(8,128)(2,1)} %get-tuple-element.25) | copy-start | bytes 9437188
  237.6 114.4 %copy-start.18 = (f32[512,20]{1,0:T(8,128)}, f32[512,20]{1,0:T(8,128)S(1)}, u32[]{:S(2)}) copy-start(f32[512,20]{1,0:T(8,128)S(1)} %get-tuple-element.52) | copy-start | bytes 122884
  516.2 440.6 %reduce-scatter.3.cloned.1.call-start = ((), (), s32[]{:S(2)}) async-start(), calls=%async_computation.5 | async-start | bytes 17694720 | tf_op jit(solution)/shard_map/reduce_scatter | solution.py:798
  522.2 116.8 %copy-start.19 = (f32[512,20]{1,0:T(8,128)S(1)}, f32[512,20]{1,0:T(8,128)}, u32[]{:S(2)}) copy-start(f32[512,20]{1,0:T(8,128)} %copy-done.18) | copy-start | bytes 122884
  523.3 118.2 %copy-start.41 = (f32[1536]{0:T(1024)S(1)}, f32[1536]{0:T(1024)}, u32[]{:S(2)}) copy-start(f32[1536]{0:T(1024)} %copy-done.40) | copy-start | bytes 18436
  523.3 118.2 %copy-start.43 = (f32[512]{0:T(512)S(1)}, f32[512]{0:T(512)}, u32[]{:S(2)}) copy-start(f32[512]{0:T(512)} %copy-done.42) | copy-start | bytes 6148
  677.1 23.3 %copy-start.22 = (bf16[512,8,3,32]{0,3,2,1:T(8,128)(2,1)S(1)}, bf16[512,8,3,32]{0,3,2,1:T(8,128)(2,1)}, u32[]{:S(2)}) copy-start(bf16[512,8,3,32]{0,3,2,1:T(8,128)(2,1)} %copy-done.21) | copy-start | bytes 2359300
  677.1 23.3 %copy-start.24 = (bf16[512,8,3,32]{0,3,2,1:T(8,128)(2,1)S(1)}, bf16[512,8,3,32]{0,3,2,1:T(8,128)(2,1)}, u32[]{:S(2)}) copy-start(bf16[512,8,3,32]{0,3,2,1:T(8,128)(2,1)} %copy-done.23) | copy-start | bytes 2359300
  709.2 19.9 %copy-start.35 = (bf16[512,8,64]{0,2,1:T(8,128)(2,1)}, bf16[512,8,64]{0,2,1:T(8,128)(2,1)S(1)}, u32[]{:S(2)}) copy-start(bf16[512,8,64]{0,2,1:T(8,128)(2,1)S(1)} %pad_maximum_fusion.5) | copy-start | bytes 1572868
  717.0 12.1 %copy-start.30 = (bf16[512,8,3,64]{0,3,2,1:T(8,128)(2,1)}, bf16[512,8,3,64]{0,3,2,1:T(8,128)(2,1)S(1)}, u32[]{:S(2)}) copy-start(bf16[512,8,3,64]{0,3,2,1:T(8,128)(2,1)S(1)} %pad_maximum_fusion.2) | copy-start | bytes 4718596
  717.0 12.1 %copy-start.14 = (bf16[1,512,1536]{2,1,0:T(8,128)(2,1)S(1)}, bf16[1,512,1536]{2,1,0:T(8,128)(2,1)}, u32[]{:S(2)}) copy-start(bf16[1,512,1536]{2,1,0:T(8,128)(2,1)} %param.11) | copy-start | bytes 4718596
  717.0 12.1 %copy-start.45 = (f32[1536]{0:T(1024)S(1)}, f32[1536]{0:T(1024)}, u32[]{:S(2)}) copy-start(f32[1536]{0:T(1024)} %copy-done.44) | copy-start | bytes 18436
  717.1 12.1 %copy-start.48 = (f32[512]{0:T(512)S(1)}, f32[512]{0:T(512)}, u32[]{:S(2)}) copy-start(f32[512]{0:T(512)} %copy-done.47) | copy-start | bytes 6148
  729.2 12.4 %copy-start.15 = (bf16[1,512,1536]{2,1,0:T(8,128)(2,1)S(1)}, bf16[1,512,1536]{2,1,0:T(8,128)(2,1)}, u32[]{:S(2)}) copy-start(bf16[1,512,1536]{2,1,0:T(8,128)(2,1)} %param.11) | copy-start | bytes 4718596
  948.5 12.2 %copy-start.1 = (bf16[384,1536]{1,0:T(8,128)(2,1)S(1)}, bf16[384,1536]{1,0:T(8,128)(2,1)}, u32[]{:S(2)}) copy-start(bf16[384,1536]{1,0:T(8,128)(2,1)} %param.16) | copy-start | bytes 3538948
  (31 other events, 181.6 us)
Sparse Core Ops, SparseCore 0:
  10.9 80.8 all-gather.3
  93.7 86.2 all-gather.7
  182.0 52.0 all-gather.5
  516.3 66.4 reduce-scatter.4
  586.2 107.3 reduce-scatter.2

commit v2 on v1

--- a/solution.py
+++ b/solution.py
@@ -25,19 +25,6 @@
     frequency = jnp.exp(jnp.arange(half_width, dtype=F32) * (-math.log(10000.0) / half_width))
     angles = jnp.arange(length, dtype=F32)[:, None] * frequency[None, :]
     return (jnp.cos(angles), jnp.sin(angles))
-
-
-def rotate(value_rows, cosine, sine_table):
-    half_width = value_rows.shape[-1] // 2
-    front_half = value_rows[..., :half_width]
-    back_half = value_rows[..., half_width:]
-    return jnp.concatenate(
-        [
-            front_half * cosine - back_half * sine_table,
-            back_half * cosine + front_half * sine_table,
-        ],
-        -1,
-    )
 
 
 def norm_apply(value_rows, gain_vec):
@@ -57,41 +44,6 @@
 
 def dot(spec, a, b):
     return jnp.einsum(spec, a, b, preferred_element_type=F32)
-
-
-def masked_scores(query_rows, key_rows_all, length, scale_factor):
-    sequence_length = query_rows.shape[0]
-    scores = dot("qgrh,kgh->grqk", query_rows, key_rows_all) * scale_factor
-    position = jnp.arange(sequence_length)
-    allowed = (position[None, :] <= position[:, None]) & (position[None, :] < length)
-    return jnp.where(allowed, scores, MASKED)
-
-
-def attend_forward(query_rows, key_rows_all, value_rows, length, scale_factor):
-    scores = masked_scores(query_rows, key_rows_all, length, scale_factor)
-    topmost = jnp.max(scores, -1, keepdims=True)
-    exponent = jnp.exp(scores - topmost)
-    totals = jnp.sum(exponent, -1, keepdims=True)
-    weights = (exponent / totals).astype(BF16)
-    mixed_heads = dot("grqk,kgh->qgrh", weights, value_rows)
-    return (
-        mixed_heads.astype(BF16).reshape(query_rows.shape[0], -1),
-        topmost + jnp.log(totals),
-    )
-
-
-def attend_backward(query_rows, key_rows_all, value_rows, length, log_total, upstream, scale_factor):
-    scores = masked_scores(query_rows, key_rows_all, length, scale_factor)
-    weights = jnp.exp(scores - log_total)
-    upstream_heads = upstream.reshape(query_rows.shape)
-    weight_grad = dot("qgrh,kgh->grqk", upstream_heads, value_rows)
-    score_grad = (
-        weights * (weight_grad - jnp.sum(weights * weight_grad, -1, keepdims=True))
-    ).astype(BF16)
-    query_grad = dot("grqk,kgh->qgrh", score_grad, key_rows_all) * scale_factor
-    key_grad = dot("grqk,qgrh->kgh", score_grad, query_rows) * scale_factor
-    value_grad = dot("grqk,qgrh->kgh", weights.astype(BF16), upstream_heads)
-    return (query_grad, key_grad, value_grad)
 
 
 def split_two(values):
@@ -351,7 +303,7 @@
     return out.at[tuple(place) + (slice(None), slice(start, stop))]
 
 
-def fan_out(arrays, lead, dp_index, bits, send, recv):
+def fan_out(arrays, lead, dp_index, bits, send, recv, between=None):
     def copy(slot, ref, bit, known, start, stop):
         place = lead + [
             slice(None) if one in known else bit_of(dp_index, one)
@@ -385,6 +337,8 @@
             one.start()
         for one in going:
             one.wait()
+        if stage == bits - 2 and between is not None:
+            between()
 
 
 def reduce_all(grads, blocks, owners, dp_size, collective):
@@ -546,13 +500,48 @@
     return sums, results[count:]
 
 
+def stream_sides(stream, block, me, owners, send, recv):
+    def source_of(step, origin):
+        return block if step == 0 else stream.at[origin]
+
+    return line_sends(me, owners, source_of, lambda origin: stream.at[origin], send, recv, 0)
+
+
+def stream_start(step, sides, owners):
+    for behind, copy in sides:
+
+        @pl.when((behind >= step) & (behind < owners - 1))
+        def _():
+            copy(step).start()
+
+
+def stream_arrive(step, sides):
+    for behind, copy in sides:
+
+        @pl.when(behind >= step + 1)
+        def _():
+            copy(step).wait_recv()
+
+
+def stream_sent(step, sides, owners):
+    for behind, copy in sides:
+
+        @pl.when((behind >= step) & (behind < owners - 1))
+        def _():
+            copy(step).wait_send()
+
+
+def line_semaphores(owners):
+    return [pltpu.SemaphoreType.DMA((1, 2, owners - 1)), pltpu.SemaphoreType.DMA((1, 2, owners - 1))]
+
+
 def gather_rows(piece, block, owners, dp_size, collective):
     bits = dp_size.bit_length() - 1
     rows, width = piece.shape[0] // dp_size, piece.shape[1]
     shape = (owners,) + (2,) * bits + (rows, width)
 
-    def kernel(piece_ref, block_ref, out, near, *scratch):
-        line_send, line_recv, near_send, near_recv, fan_send, fan_recv, local = scratch
+    def kernel(piece_ref, block_ref, out, stream, *scratch):
+        line_send, line_recv, stream_send, stream_recv, fan_send, fan_recv, local = scratch
         me, dp_index = lax.axis_index("expert"), lax.axis_index("dp")
         greet_all(me, owners, dp_index, bits)
         place = tuple(bit_of(dp_index, bit) for bit in range(bits - 1, -1, -1))
@@ -565,80 +554,259 @@
             return out.at[(origin,) + place]
 
         sides = line_sends(me, owners, source_of, target_of, line_send, line_recv, 0)
-        keep = pltpu.make_async_copy(mine, out.at[(me,) + place], local)
+        far = stream_sides(stream, block_ref, me, owners, stream_send, stream_recv)
+        keep = pltpu.make_async_copy(mine, out.at[(me,) + place], local.at[0])
+        stay = pltpu.make_async_copy(block_ref, stream.at[me], local.at[1])
         for step in range(owners):
             line_step(step, sides, owners)
             if step == 0:
                 keep.start()
+        stream_start(0, far, owners)
+        stay.start()
         keep.wait()
 
-        def nearby(side):
-            return pltpu.make_async_remote_copy(
-                src_ref=block_ref,
-                dst_ref=near.at[side],
-                send_sem=near_send.at[side],
-                recv_sem=near_recv.at[side],
-                device_id={"expert": me + 1 - 2 * side},
-                device_id_type=MESH,
-            )
-
-        ahead = (owners - 1 - me, me)
-        for side in range(2):
-
-            @pl.when(ahead[side] > 0)
-            def _():
-                nearby(side).start()
-
-        fan_out([out], [slice(None)], dp_index, bits, fan_send, fan_recv)
+        def between():
+            stream_arrive(0, far)
+            stream_start(1, far, owners)
+
+        fan_out([out], [slice(None)], dp_index, bits, fan_send, fan_recv, between)
         line_finish(sides, owners)
-        for side in range(2):
-
-            @pl.when(ahead[side] > 0)
-            def _():
-                nearby(side).wait_send()
-
-            @pl.when(ahead[1 - side] > 0)
-            def _():
-                nearby(side).wait_recv()
-
-    full, near = pl.pallas_call(
+        stay.wait()
+        stream_sent(0, far, owners)
+        stream_arrive(1, far)
+        stream_sent(1, far, owners)
+
+    full, stream = pl.pallas_call(
         kernel,
         out_shape=[
             jax.ShapeDtypeStruct(shape, BF16),
-            jax.ShapeDtypeStruct((2,) + block.shape, BF16),
+            jax.ShapeDtypeStruct((owners,) + block.shape, BF16),
         ],
         in_specs=[vmem_spec()] * 2,
         out_specs=[any_spec()] * 2,
-        scratch_shapes=[
-            pltpu.SemaphoreType.DMA((1, 2, owners - 1)),
-            pltpu.SemaphoreType.DMA((1, 2, owners - 1)),
-            pltpu.SemaphoreType.DMA((2,)),
-            pltpu.SemaphoreType.DMA((2,)),
+        scratch_shapes=line_semaphores(owners)
+        + line_semaphores(owners)
+        + [
             pltpu.SemaphoreType.DMA((2 * bits - 1,)),
             pltpu.SemaphoreType.DMA((2 * bits - 1,)),
-            pltpu.SemaphoreType.DMA,
+            pltpu.SemaphoreType.DMA((2,)),
         ],
         compiler_params=kernel_params(collective),
     )(piece.reshape((2,) * bits + (rows, width)), block)
-    return full.reshape(owners * dp_size * rows, width), near
-
-
-def permute_gather(block, near, owner, owners):
-    right, left = near[0], near[1]
-    rightward, leftward = [right], [left]
-    for step in range(1, owners - 1):
-        right = lax.ppermute(right, "expert", [(z, z + 1) for z in range(step, owners - 1)])
-        left = lax.ppermute(left, "expert", [(z, z - 1) for z in range(1, owners - step)])
-        rightward.append(right)
-        leftward.append(left)
-    blocks = [block] + [
-        jnp.where(owner + k < owners, leftward[k - 1], rightward[owners - k - 1])
-        for k in range(1, owners)
+    return full.reshape(owners * dp_size * rows, width), stream
+
+
+def lane_below(shape, bound, period):
+    return lax.rem(lax.broadcasted_iota(jnp.int32, shape, len(shape) - 1), period) < bound
+
+
+def swing(values, cosine, sine):
+    width = values.shape[1]
+    half = HEAD_SIZE // 2
+    front = lane_below(values.shape, half, HEAD_SIZE)
+    other = jnp.where(
+        front, -pltpu.roll(values, width - half, 1), pltpu.roll(values, half, 1)
+    )
+    times = width // 128
+    return values * jnp.tile(cosine, (1, times)) + other * jnp.tile(sine, (1, times))
+
+
+def contract(a, b, axis_a, axis_b):
+    return lax.dot_general(
+        a, b, (((axis_a,), (axis_b,)), ((), ())), preferred_element_type=F32
+    )
+
+
+def head_tiles(natural):
+    front = lane_below(natural.shape, HEAD_SIZE, 128)
+    wide = natural.astype(F32)
+    turned = pltpu.roll(wide, HEAD_SIZE, 1)
+    return [
+        jnp.where(front, wide, turned).astype(BF16),
+        natural,
+        jnp.where(front, turned, wide).astype(BF16),
     ]
-    whole = jnp.concatenate(blocks + blocks, 0)
-    return lax.dynamic_slice_in_dim(
-        whole, lax.rem(owners - owner, owners) * block.shape[0], owners * block.shape[0], 0
-    ).reshape((owners,) + block.shape)
+
+
+def masked_weights(query, key, start, stop, length, scale_factor):
+    scores = contract(query, key[:stop], 1, 1) * scale_factor
+    rows = start + lax.broadcasted_iota(jnp.int32, scores.shape, 0)
+    columns = lax.broadcasted_iota(jnp.int32, scores.shape, 1)
+    scores = jnp.where((columns <= rows) & (columns < length), scores, MASKED)
+    exponent = jnp.exp(scores - jnp.max(scores, -1, keepdims=True))
+    return exponent / jnp.sum(exponent, -1, keepdims=True)
+
+
+def row_tiles(length):
+    size = 256 if length % 256 == 0 else length
+    return [(start, start + size) for start in range(0, length, size)]
+
+
+def attention_forward(projected_ref, cosine_ref, sine_ref, length, rotated_ref, attended_ref, pair):
+    scale_factor = HEAD_SIZE ** (-0.5)
+    count = projected_ref.shape[0]
+    query_width = QUERY_HEADS * HEAD_SIZE
+    key_width = KEY_VALUE_HEADS * HEAD_SIZE
+
+    def columns(start, width):
+        return pl.ds(pl.multiple_of(start + pair * width, 128), width)
+
+    cosine, sine = cosine_ref[...], sine_ref[...]
+    query_at, key_at = columns(0, 384), columns(query_width, 128)
+    value_at = columns(query_width + key_width, 128)
+    query = swing(projected_ref[:, query_at], cosine, sine).astype(BF16)
+    key = swing(projected_ref[:, key_at], cosine, sine).astype(BF16)
+    value = projected_ref[:, value_at].astype(BF16)
+    rotated_ref[:, query_at] = query
+    rotated_ref[:, key_at] = key
+    rotated_ref[:, value_at] = value
+    keys, values = head_tiles(key), head_tiles(value)
+    for tile in range(3):
+        for start, stop in row_tiles(count):
+            both = query[start:stop, tile * 128 : tile * 128 + 128]
+            front = lane_below(both.shape, HEAD_SIZE, 128)
+            parts = []
+            for side in range(2):
+                one = jnp.where(front == (side == 0), both, jnp.zeros_like(both))
+                weights = masked_weights(one, keys[tile], start, stop, length, scale_factor)
+                parts.append(contract(weights.astype(BF16), values[tile][:stop], 1, 0))
+            attended_ref[start:stop, columns_of(pair, tile)] = jnp.where(
+                front, parts[0], parts[1]
+            ).astype(BF16)
+
+
+def columns_of(pair, tile):
+    return pl.ds(pl.multiple_of(pair * 384 + tile * 128, 128), 128)
+
+
+def attention_backward(rotated_ref, grad_ref, cosine_ref, sine_ref, length, out_ref, pair):
+    scale_factor = HEAD_SIZE ** (-0.5)
+    count = rotated_ref.shape[0]
+    query_width = QUERY_HEADS * HEAD_SIZE
+    key_width = KEY_VALUE_HEADS * HEAD_SIZE
+
+    def columns(start, width):
+        return pl.ds(pl.multiple_of(start + pair * width, 128), width)
+
+    cosine, sine = cosine_ref[...], sine_ref[...]
+    key_at = columns(query_width, 128)
+    value_at = columns(query_width + key_width, 128)
+    keys, values = head_tiles(rotated_ref[:, key_at]), head_tiles(rotated_ref[:, value_at])
+    front = lane_below((count, 128), HEAD_SIZE, 128)
+    key_total = value_total = None
+    for tile in range(3):
+        key_sum = jnp.zeros((count, 128), F32)
+        value_sum = jnp.zeros((count, 128), F32)
+        for start, stop in row_tiles(count):
+            query = rotated_ref[start:stop, columns_of(pair, tile)]
+            grad = grad_ref[start:stop, columns_of(pair, tile)]
+            part = front[start:stop]
+            parts = []
+            for side in range(2):
+                chosen = part == (side == 0)
+                one = jnp.where(chosen, query, jnp.zeros_like(query))
+                rise = jnp.where(chosen, grad, jnp.zeros_like(grad))
+                weights = masked_weights(one, keys[tile], start, stop, length, scale_factor)
+                weight_grad = contract(rise, values[tile][:stop], 1, 1)
+                score_grad = (
+                    weights
+                    * (weight_grad - jnp.sum(weights * weight_grad, -1, keepdims=True))
+                ).astype(BF16)
+                parts.append(contract(score_grad, keys[tile][:stop], 1, 0))
+                key_part = contract(score_grad, one, 0, 0)
+                value_part = contract(weights.astype(BF16), rise, 0, 0)
+                if stop < count:
+                    rest = jnp.zeros((count - stop, 128), F32)
+                    key_part = jnp.concatenate([key_part, rest], 0)
+                    value_part = jnp.concatenate([value_part, rest], 0)
+                key_sum = key_sum + key_part
+                value_sum = value_sum + value_part
+            query_grad = jnp.where(part, parts[0], parts[1]) * scale_factor
+            out_ref[start:stop, columns_of(pair, tile)] = swing(
+                query_grad, cosine[start:stop], -sine[start:stop]
+            ).astype(BF16)
+        sums = []
+        for total in (key_sum, value_sum):
+            if tile != 1:
+                total = total + pltpu.roll(total, HEAD_SIZE, 1)
+                total = jnp.where(front == (tile == 0), total, jnp.zeros_like(total))
+            sums.append(total)
+        key_total = sums[0] if key_total is None else key_total + sums[0]
+        value_total = sums[1] if value_total is None else value_total + sums[1]
+    out_ref[:, key_at] = swing(key_total * scale_factor, cosine, -sine).astype(BF16)
+    out_ref[:, value_at] = value_total.astype(BF16)
+
+
+def angle_tables(length):
+    cosine, sine = tables(length, HEAD_SIZE)
+    return jnp.tile(cosine, (1, 4)), jnp.tile(sine, (1, 4))
+
+
+def smem_spec():
+    return pl.BlockSpec(memory_space=pltpu.SMEM)
+
+
+def local_params():
+    return pltpu.CompilerParams(vmem_limit_bytes=VMEM_LIMIT)
+
+
+def attend_backward(rotated, grad, cosine, sine, length):
+    count, width = rotated.shape
+
+    def kernel(length_ref, rotated_ref, grad_ref, cosine_ref, sine_ref, out_ref):
+        @pl.loop(0, KEY_VALUE_HEADS // 2)
+        def _(pair):
+            attention_backward(
+                rotated_ref, grad_ref, cosine_ref, sine_ref, length_ref[0], out_ref, pair
+            )
+
+        out_ref[:, width:] = jnp.zeros((count, AUX), BF16)
+
+    return pl.pallas_call(
+        kernel,
+        out_shape=jax.ShapeDtypeStruct((count, width + AUX), BF16),
+        in_specs=[smem_spec()] + [vmem_spec()] * 4,
+        out_specs=vmem_spec(),
+        compiler_params=local_params(),
+    )(length, rotated, grad, cosine, sine)
+
+
+def attend_forward(projected, cosine, sine, length, width, stream, owners, collective):
+    count = projected.shape[0]
+
+    def kernel(length_ref, projected_ref, cosine_ref, sine_ref, _, *refs):
+        rotated_ref, attended_ref, stream_ref, send, recv = refs
+        me = lax.axis_index("expert")
+        greet_all(me, owners, 0, 0)
+        far = stream_sides(stream_ref, None, me, owners, send, recv)
+        stream_start(2, far, owners)
+
+        @pl.loop(0, KEY_VALUE_HEADS // 2)
+        def _(pair):
+            attention_forward(
+                projected_ref, cosine_ref, sine_ref, length_ref[0], rotated_ref, attended_ref, pair
+            )
+
+        for step in range(3, owners - 1):
+            stream_arrive(step - 1, far)
+            stream_start(step, far, owners)
+        stream_arrive(owners - 2, far)
+        for step in range(2, owners - 1):
+            stream_sent(step, far, owners)
+
+    return pl.pallas_call(
+        kernel,
+        out_shape=[
+            jax.ShapeDtypeStruct((count, width), BF16),
+            jax.ShapeDtypeStruct((count, QUERY_HEADS * HEAD_SIZE), BF16),
+            jax.ShapeDtypeStruct(stream.shape, BF16),
+        ],
+        in_specs=[smem_spec()] + [vmem_spec()] * 3 + [any_spec()],
+        out_specs=[vmem_spec()] * 2 + [any_spec()],
+        scratch_shapes=line_semaphores(owners),
+        input_output_aliases={4: 2},
+        compiler_params=kernel_params(collective),
+    )(length, projected, cosine, sine, stream)
 
 
 def gather_slow(piece, dp_index, dp_size):
@@ -665,14 +833,10 @@
     owner = lax.axis_index("expert")
     dp_index = lax.axis_index("dp")
     _, length, width = tokens.shape
-    query_groups = QUERY_HEADS // KEY_VALUE_HEADS
     local_experts = expert_in.shape[0]
     experts = local_experts * owners
     capacity = length * TOPK // experts
-    scale_factor = HEAD_SIZE ** (-0.5)
-    query_width = QUERY_HEADS * HEAD_SIZE
-    key_width = KEY_VALUE_HEADS * HEAD_SIZE
-    qkv_width = query_width + 2 * key_width
+    qkv_width = (QUERY_HEADS + 2 * KEY_VALUE_HEADS) * HEAD_SIZE
 
     small = jnp.concatenate(
         [
@@ -683,11 +847,10 @@
         ],
         1,
     )
-    qkv_packed, near = gather_rows(
+    qkv_packed, stream = gather_rows(
         jnp.concatenate([query_key_value_weight, small], 1), cotangent[0], owners, dp_size, 1
     )
     out_full = gather_slow(w_out, dp_index, dp_size)
-    upstream_all = permute_gather(cotangent[0], near, owner, owners)
     small_full = qkv_packed[:, qkv_width:].astype(F32)
     router_wide = small_full[:, :experts]
     gain_first = small_full[:, experts]
@@ -701,30 +864,9 @@
     normed_first, factor_first = norm_apply(inputs, gain_first)
     normed_low = normed_first.astype(BF16)
     projected_rows = dot("td,df->tf", normed_low, qkv_packed)
-    cosine, sine_table = tables(length, HEAD_SIZE)
-    cos_four = cosine[:, None, None, :]
-    sin_four = sine_table[:, None, None, :]
-    cos_three = cosine[:, None, :]
-    sin_three = sine_table[:, None, :]
-    query_rows = rotate(
-        projected_rows[:, :query_width].reshape(length, KEY_VALUE_HEADS, query_groups, HEAD_SIZE),
-        cos_four,
-        sin_four,
-    ).astype(BF16)
-    key_rows_all = rotate(
-        projected_rows[:, query_width : query_width + key_width].reshape(
-            length, KEY_VALUE_HEADS, HEAD_SIZE
-        ),
-        cos_three,
-        sin_three,
-    ).astype(BF16)
-    value_rows = (
-        projected_rows[:, query_width + key_width : qkv_width]
-        .reshape(length, KEY_VALUE_HEADS, HEAD_SIZE)
-        .astype(BF16)
-    )
-    attended, log_total = attend_forward(
-        query_rows, key_rows_all, value_rows, sequence_live, scale_factor
+    cosine, sine_table = angle_tables(length)
+    rotated, attended, upstream_all = attend_forward(
+        projected_rows, cosine, sine_table, seq_lengths, qkv_width, stream, owners, 6
     )
     hidden_sum = inputs + dot("ti,id->td", attended, out_full)
     normed_second, factor_second = norm_apply(hidden_sum, gain_second)
@@ -818,20 +960,7 @@
     total_low = total_grad.astype(BF16)
     out_weight_grad = dot("ti,td->id", attended, total_low)
     attended_grad = dot("td,id->ti", total_low, out_full).astype(BF16)
-    query_grad, key_grad, value_grad = attend_backward(
-        query_rows, key_rows_all, value_rows, sequence_live, log_total, attended_grad, scale_factor
-    )
-    query_grad = rotate(query_grad, cos_four, -sin_four)
-    key_grad = rotate(key_grad, cos_three, -sin_three)
-    projected_grad = jnp.concatenate(
-        [
-            query_grad.reshape(length, -1),
-            key_grad.reshape(length, -1),
-            value_grad.reshape(length, -1),
-            jnp.zeros((length, AUX), F32),
-        ],
-        -1,
-    ).astype(BF16)
+    projected_grad = attend_backward(rotated, attended_grad, cosine, sine_table, seq_lengths)
     qkv_weight_grad = dot("td,tf->df", normed_low, projected_grad)
     first_grad = dot("tf,df->td", projected_grad, qkv_packed)
     input_back, gain_one_grad = norm_back(inputs, factor_first, gain_first, first_grad)

time: 976 us -> 890 us (0.912)
  Pallas kernels: 473 us -> 578 us
  matrix products: 293 us -> 219 us
  other arithmetic: 97.5 us -> 41 us
  waiting for transfers between devices: 30.6 us -> 1.97 us
  local copies, waits for them, and re-layouts: 51.2 us -> 25.1 us
    pallas_call x0 -> x2, Pallas kernels: none -> 79.1 us  [the longest x1 40.5 us: attend_forward(): pl.pallas_call(kernel, out_shape=[jax.ShapeDtypeStruct((count, width), BF...]
    dot_general x22 -> x16, matrix products: 285 us -> 211 us  [dot(): return jnp.einsum(spec, a, b, preferred_element_type=F32)]
    pallas_call x1, Pallas kernels: 83.7 us -> 116 us  [gather_rows(): pl.pallas_call(kernel, out_shape=[jax.ShapeDtypeStruct(shape, BF16), jax....]
    ppermute x4 -> x0, waiting for transfers between devices: 29.3 us -> none  [the longest x2 29.3 us: permute_gather(): lax.ppermute(left, 'expert', [(z, z - 1) for z in range(1, owners - step)])]
    convert_element_type x1 -> x0, other arithmetic: 23.2 us -> none  [attend_backward(): score_grad = (weights * (weight_grad - jnp.sum(weights * weight_grad, -1,...]
    unnamed x6 -> x1, other arithmetic: 13.7 us -> 0.01 us
    reduce_sum x1 -> x0, other arithmetic: 11.3 us -> none  [attend_forward(): totals = jnp.sum(exponent, -1, keepdims=True)]
  transfers between devices with their start and end apart: 9 -> 5, of which waited for: 1 -> 0; matrix products, arithmetic and copies ran while one was open for 33% -> 19% of each run, Pallas kernels for 49% -> 66%
where the time goes in v2:
time: 890 us; the launch traced here: 882 us
  Pallas kernels  578 us (65%)
  matrix products  219 us (25%)
  other arithmetic  41 us (5%)
  local copies, waits for them, and re-layouts  25.1 us (3%)
  between operations  15.3 us (2%)
    dot_general x16, matrix products, dot(): return jnp.einsum(spec, a, b, preferred_element_type=F32)  211 us
    pallas_call x1, Pallas kernels, reduce_all(): pl.pallas_call(kernel, out_shape=[jax.ShapeDtypeStruct((2,) * bits + shap...  160 us
    pallas_call x1, Pallas kernels, gather_rows(): pl.pallas_call(kernel, out_shape=[jax.ShapeDtypeStruct(shape, BF16), jax....  116 us
    pallas_call x1, Pallas kernels, line_scatter(): pl.pallas_call(kernel, out_shape=[jax.ShapeDtypeStruct(b.shape[1:], F32)...  113 us
    pallas_call x1, Pallas kernels, line_gather(): pl.pallas_call(kernel, out_shape=[jax.ShapeDtypeStruct((owners,) + b.shap...  112 us
    pallas_call x1, Pallas kernels, attend_forward(): pl.pallas_call(kernel, out_shape=[jax.ShapeDtypeStruct((count, width), BF...  40.5 us
    pallas_call x1, Pallas kernels, attend_backward(): pl.pallas_call(kernel, out_shape=jax.ShapeDtypeStruct((count, width + AUX...  38.5 us
  transfers between devices with their start and end apart: 5, of which 0 were waited for; matrix products, arithmetic and copies ran while one was open for 19% of the time, Pallas kernels for 66%

profile of v2, /device:TPU:0, one launch (start us, length us, event | category | flops | bytes accessed | tf_op | source)
XLA Modules:
  0.0 881.5 jit_solution(317456689429590107)
XLA Ops:
  14.1 3.0 concatenate.30.piece_ref
  17.1 115.5 %shard_map.178 = (bf16[4,2,2,2,48,2688]{5,4,3,2,1,0:T(8,128)(2,1)}, bf16[4,512,1536]{2,1,0:T(8,128)(2,1)}) custom-call(bf16[2,2,2,48,2688]{4,3,2,1,0:T(8,128)(2,1)} %concatenate.30.piece_ref, bf16[512,1536]{1,0:T(8,128)(2,1)} %bitcast.128), custom_call_target="tpu_custom_call" | custom-call | tf_op jit(solution)/shard_map/pallas_call | solution.py:579
  136.8 9.9 %fusion.59.projected_ref = f32[512,2688]{1,0:T(8,128)} fusion(bf16[1536,2688]{1,0:T(8,128)(2,1)} %bitcast.136, bf16[1,512,1536]{2,1,0:T(8,128)(2,1)S(1)} %copy-done.10, f32[1536]{0:T(1024)S(1)} %get-tuple-element.50, f32[512]{0:T(512)S(1)} %add_rsqrt_fusion.1), kind=kOutput, calls=%fused_computation.75 | convolution fusion | flops 4231004160 | bytes 15343616 | tf_op jit(solution)/shard_map/td,df->tf/dot_general | solution.py:46
  146.7 40.5 %shard_map.179 = (bf16[512,2560]{1,0:T(8,128)(2,1)}, bf16[512,1536]{1,0:T(8,128)(2,1)}, bf16[4,512,1536]{2,1,0:T(8,128)(2,1)}) custom-call(s32[1]{0:T(128)} %copy.181.length_ref, f32[512,2688]{1,0:T(8,128)} %fusion.59.projected_ref, f32[512,128]{1,0:T(8,128)} %copy.119.cosine_ref, f32[512,128]{1,0:T(8,128)} %copy.120.sine_ref, ...), custom_call_target="tpu_custom_call", output_to_operand_aliasing={{2}: (4, {})} | custom-call | tf_op jit(solution)/shard_map/pallas_call | solution.py:797
  187.7 5.5 multiply_reduce_fusion.3
  198.6 111.6 %shard_map.180 = (bf16[4,512,1536]{2,1,0:T(8,128)(2,1)}, bf16[4,512,128]{2,1,0:T(8,128)(2,1)}) custom-call(bf16[512,1536]{1,0:T(8,128)(2,1)} %copy-done.4, bf16[512,128]{1,0:T(8,128)(2,1)} %maximum_maximum_fusion.1.refs_1_), custom_call_target="tpu_custom_call" | custom-call | tf_op jit(solution)/shard_map/pallas_call | solution.py:173
  312.8 12.5 %convert_bitcast_fusion = bf16[5,4,204,1536]{3,2,0,1:T(8,128)(2,1)} fusion(bf16[4,512,1536]{2,1,0:T(8,128)(2,1)} %get-tuple-element.32, f32[4,5,512]{2,1,0:T(8,128)S(1)} %copy.127), kind=kOutput, calls=%fused_computation.11 | convolution fusion | flops 6425640960 | bytes 18866176 | tf_op jit(solution)/shard_map/sect,std->escd/dot_general | solution.py:46
  325.3 12.4 %convert_bitcast_fusion.1 = bf16[5,4,204,1536]{3,2,0,1:T(8,128)(2,1)} fusion(bf16[4,512,1536]{2,1,0:T(8,128)(2,1)} %get-tuple-element.31, f32[4,5,512]{2,1,0:T(8,128)S(1)} %copy.127), kind=kOutput, calls=%fused_computation.12 | convolution fusion | flops 6425640960 | bytes 18866176 | tf_op jit(solution)/shard_map/sect,std->escd/dot_general | solution.py:46
  337.7 24.1 %fusion = f32[5,4,204,1024]{3,2,1,0:T(8,128)} fusion(bf16[5,1536,1024]{2,1,0:T(8,128)(2,1)} %all-gather.8.cloned.1.call-done, bf16[5,4,204,1536]{3,2,0,1:T(8,128)(2,1)} %convert_bitcast_fusion), kind=kOutput, calls=%fused_computation.1 | convolution fusion | flops 12834570240 | bytes 44974080 | tf_op jit(solution)/shard_map/escd,edf->escf/dot_general | solution.py:46
  361.8 17.3 %multiply_reduce_fusion = (f32[5,4,204]{2,1,0:T(4,128)S(1)}, f32[5,4,204,512]{3,2,1,0:T(8,128)S(1)}) fusion(f32[5,4,204,1024]{3,2,1,0:T(8,128)} %fusion, bf16[5,512,1536]{2,1,0:T(8,128)(2,1)} %all-gather.6.cloned.1.call-done, bf16[5,4,204,1536]{3,2,0,1:T(8,128)(2,1)} %convert_bitcast_fusion.1), kind=kOutput, calls=%fused_computation.22 | convolution fusion | flops 6436081664 | bytes 45481920 | tf_op jit(solution)/shard_map/escd,ehd->esch/dot_general | solution.py:46
  379.1 2.4 select_reduce_fusion
  381.5 12.3 %multiply_convert_fusion.2 = (bf16[5,4,204,512]{3,2,1,0:T(8,128)(2,1)}, bf16[5,4,204,512]{3,2,1,0:T(8,128)(2,1)}, bf16[5,4,204,512]{3,2,1,0:T(8,128)(2,1)}) fusion(f32[5,4,204,1024]{3,2,1,0:T(8,128)} %fusion, f32[5,4,204,512]{3,2,1,0:T(8,128)S(1)} %get-tuple-element.71, f32[5,4,204]{2,1,0:T(4,128)S(1)} %copy.130), kind=kLoop, calls=%fused_computation.25 | loop fusion | flops 35512320 | bytes 37617600 | tf_op jit(solution)/shard_map/convert.9
  393.9 24.2 %bitcast_convert_fusion = bf16[5,1536,1024]{2,1,0:T(8,128)(2,1)} fusion(bf16[5,4,204,1536]{3,2,0,1:T(8,128)(2,1)} %convert_bitcast_fusion, bf16[5,4,204,512]{3,2,1,0:T(8,128)(2,1)} %get-tuple-element.60, bf16[5,4,204,512]{3,2,1,0:T(8,128)(2,1)} %get-tuple-element.59), kind=kOutput, calls=%fused_computation | convolution fusion | flops 12859146240 | bytes 36618240 | tf_op jit(solution)/shard_map/escd,escf->edf/dot_general | solution.py:46
  418.0 24.9 %fusion.2 = bf16[5,4,204,1536]{3,2,0,1:T(8,128)(2,1)} fusion(bf16[5,1536,1024]{2,1,0:T(8,128)(2,1)} %all-gather.8.cloned.1.call-done, bf16[5,4,204,512]{3,2,1,0:T(8,128)(2,1)} %get-tuple-element.60, bf16[5,4,204,512]{3,2,1,0:T(8,128)(2,1)} %get-tuple-element.59), kind=kOutput, calls=%fused_computation.4 | convolution fusion | flops 12851281920 | bytes 36618240 | tf_op jit(solution)/shard_map/escf,edf->escd/dot_general | solution.py:46
  442.9 15.3 %bitcast_convert_fusion.3.refs_0_ = bf16[4,512,1536]{2,1,0:T(8,128)(2,1)} fusion(bf16[5,4,204,1536]{3,2,0,1:T(8,128)(2,1)} %fusion.2, f32[4,5,512]{2,1,0:T(8,128)S(1)} %copy.127), kind=kOutput, calls=%fused_computation.14 | convolution fusion | flops 6422519808 | bytes 18866176 | tf_op jit(solution)/shard_map/sect,escd->std/dot_general | solution.py:46
  458.3 15.1 %bitcast_convert_fusion.1 = bf16[5,512,1536]{2,1,0:T(8,128)(2,1)} fusion(bf16[5,4,204,512]{3,2,1,0:T(8,128)(2,1)S(1)} %copy-done.12, bf16[5,4,204,1536]{3,2,0,1:T(8,128)(2,1)} %convert_bitcast_fusion.1), kind=kOutput, calls=%fused_computation.3 | convolution fusion | flops 6421217280 | bytes 24576000 | tf_op jit(solution)/shard_map/esch,escd->ehd/dot_general | solution.py:46
  474.7 4.2 dynamic_update_slice.6
  480.2 112.6 %shard_map.181 = (f32[512,1536]{1,0:T(8,128)}, f32[512,128]{1,0:T(8,128)}) custom-call(bf16[4,512,1536]{2,1,0:T(8,128)(2,1)} %bitcast_convert_fusion.3.refs_0_, bf16[4,512,128]{2,1,0:T(8,128)(2,1)} %maximum_maximum_fusion.refs_1_), custom_call_target="tpu_custom_call" | custom-call | tf_op jit(solution)/shard_map/pallas_call | solution.py:283
  595.4 5.9 multiply_reduce_fusion.1
  602.7 3.7 convolution_convert_fusion.2.grad_ref
  606.5 38.5 %shard_map.182 = bf16[512,2688]{1,0:T(8,128)(2,1)} custom-call(s32[1]{0:T(128)} %copy.181.length_ref, bf16[512,2560]{1,0:T(8,128)(2,1)} %get-tuple-element.29.rotated_ref, bf16[512,1536]{1,0:T(8,128)(2,1)} %convolution_convert_fusion.2.grad_ref, f32[512,128]{1,0:T(8,128)} %copy.119.cosine_ref, f32[512,128]{1,0:T(8,128)} %copy.120.sine_ref), custom_call_target="tpu_custom_call" | custom-call | tf_op jit(solution)/shard_map/pallas_call | solution.py:765
  645.0 10.8 %fusion.49 = (f32[512]{0:T(512)S(1)}, bf16[1536]{0:T(1024)(128)(2,1)S(1)}, f32[512,1536]{1,0:T(8,128)}) fusion(bf16[1,512,1536]{2,1,0:T(8,128)(2,1)S(1)} %copy-done.11, f32[1536]{0:T(1024)S(1)} %copy-done.23, f32[512]{0:T(512)S(1)} %copy-done.26, bf16[512,2688]{1,0:T(8,128)(2,1)} %shard_map.182, bf16[1536,2688]{1,0:T(8,128)(2,1)} %bitcast.139), kind=kOutput, calls=%fused_computation.56 | convolution fusion | flops 4233361408 | bytes 15741952 | tf_op jit(solution)/shard_map/tf,df->td/dot_general | solution.py:46
  657.2 9.2 %convolution_convert_fusion = bf16[1536,2688]{1,0:T(8,128)(2,1)} fusion(bf16[512,2688]{1,0:T(8,128)(2,1)} %shard_map.182, bf16[1,512,1536]{2,1,0:T(8,128)(2,1)S(1)} %copy-done.11, f32[1536]{0:T(1024)S(1)} %copy-done.23, f32[512]{0:T(512)S(1)} %copy-done.26), kind=kOutput, calls=%fused_computation.15 | convolution fusion | flops 4235132928 | bytes 12591104 | tf_op jit(solution)/shard_map/td,tf->df/dot_general | solution.py:46
  667.6 4.3 convolution_convert_fusion.1
  671.9 21.2 %bitcast_convert_fusion.2.refs_2_ = bf16[4,512,1536]{2,1,0:T(8,128)(2,1)} fusion(f32[4,5,512]{2,1,0:T(8,128)S(1)} %copy.127, bf16[5,512,1536]{2,1,0:T(8,128)(2,1)} %all-gather.6.cloned.1.call-done, bf16[5,4,204,512]{3,2,1,0:T(8,128)(2,1)} %get-tuple-element.37), kind=kOutput, calls=%fused_computation.13 | convolution fusion | flops 12846071808 | bytes 18374656 | tf_op jit(solution)/shard_map/sect,escd->std/dot_general | solution.py:46
  693.1 159.7 %shard_map.183 = (bf16[2,2,2,48,2688]{4,3,2,1,0:T(8,128)(2,1)}, bf16[2,2,2,48,1536]{4,3,2,1,0:T(8,128)(2,1)}, f32[512,1536]{1,0:T(8,128)}) custom-call(bf16[4,2,2,2,48,2688]{5,4,3,2,1,0:T(8,128)(2,1)} %bitcast.30.refs_0_, bf16[4,2,2,2,48,1536]{5,4,3,2,1,0:T(8,128)(2,1)} %bitcast.129, bf16[4,512,1536]{2,1,0:T(8,128)(2,1)} %bitcast_convert_fusion.2.refs_2_), custom_call_target="tpu_custom_call" | custom-call | tf_op jit(solution)/shard_map/pallas_call | solution.py:488
  852.9 1.8 bitcast_convert_fusion.4
  854.7 2.4 slice.56
  858.7 2.1 slice_reduce_fusion
  862.5 5.6 fusion.57
  868.1 2.7 convert_element_type.182
  870.8 3.9 convert_element_type.181
  (135 shorter events, 30.9 us)
Async XLA Ops:
  7.2 6.9 copy-start.16
  7.2 180.5 %all-gather.4.cloned.1.call-start = ((), (), s32[]{:S(2)}) async-start(), calls=%async_computation.2 | async-start | bytes 4866048 | tf_op jit(solution)/shard_map/all_gather | solution.py:815
  9.2 328.5 %all-gather.8.cloned.1.call-start = ((), (), s32[]{:S(2)}) async-start(), calls=%async_computation.4 | async-start | bytes 17694720 | tf_op jit(solution)/shard_map/all_gather | solution.py:905
  9.9 351.9 %all-gather.6.cloned.1.call-start = ((), (), s32[]{:S(2)}) async-start(), calls=%async_computation.3 | async-start | bytes 8847360 | tf_op jit(solution)/shard_map/all_gather | solution.py:906
  10.6 857.5 %reduce-scatter.5.cloned.1.call-start = ((), (), s32[]{:S(2)}) async-start(), calls=%async_computation.6 | async-start | bytes 8847360 | tf_op jit(solution)/shard_map/reduce_scatter | solution.py:943
  17.1 118.9 %copy-start.24 = (s32[1,512,8]{1,2,0:T(8,128)S(1)}, s32[1,512,8]{1,2,0:T(8,128)}, u32[]{:S(2)}) copy-start(s32[1,512,8]{1,2,0:T(8,128)} %param.13) | copy-start | bytes 49156
  17.1 119.3 %copy-start.10 = (bf16[1,512,1536]{2,1,0:T(8,128)(2,1)S(1)}, bf16[1,512,1536]{2,1,0:T(8,128)(2,1)}, u32[]{:S(2)}) copy-start(bf16[1,512,1536]{2,1,0:T(8,128)(2,1)} %param.11) | copy-start | bytes 4718596
  136.3 10.3 %copy-start.22 = (f32[1536]{0:T(1024)}, f32[1536]{0:T(1024)S(1)}, u32[]{:S(2)}) copy-start(f32[1536]{0:T(1024)S(1)} %get-tuple-element.50) | copy-start | bytes 18436
  136.3 56.9 %copy-start.18 = (f32[1536]{0:T(1024)}, f32[1536]{0:T(1024)S(1)}, u32[]{:S(2)}) copy-start(f32[1536]{0:T(1024)S(1)} %get-tuple-element.49) | copy-start | bytes 18436
  136.8 9.9 %copy-start.25 = (f32[512]{0:T(512)}, f32[512]{0:T(512)S(1)}, u32[]{:S(2)}) copy-start(f32[512]{0:T(512)S(1)} %add_rsqrt_fusion.1) | copy-start | bytes 6148
  193.2 1.7 copy-start.2
  195.2 3.3 copy-start.4
  197.7 112.5 %copy-start.13 = (f32[512,20]{1,0:T(8,128)}, f32[512,20]{1,0:T(8,128)S(1)}, u32[]{:S(2)}) copy-start(f32[512,20]{1,0:T(8,128)S(1)} %get-tuple-element.58) | copy-start | bytes 122884
  442.9 15.3 %copy-start.12 = (bf16[5,4,204,512]{3,2,1,0:T(8,128)(2,1)S(1)}, bf16[5,4,204,512]{3,2,1,0:T(8,128)(2,1)}, u32[]{:S(2)}) copy-start(bf16[5,4,204,512]{3,2,1,0:T(8,128)(2,1)} %get-tuple-element.37) | copy-start | bytes 12533764
  473.5 397.4 %reduce-scatter.3.cloned.1.call-start = ((), (), s32[]{:S(2)}) async-start(), calls=%async_computation.5 | async-start | bytes 17694720 | tf_op jit(solution)/shard_map/reduce_scatter | solution.py:940
  479.1 113.7 %copy-start.14 = (f32[512,20]{1,0:T(8,128)S(1)}, f32[512,20]{1,0:T(8,128)}, u32[]{:S(2)}) copy-start(f32[512,20]{1,0:T(8,128)} %copy-done.13) | copy-start | bytes 122884
  480.2 115.1 %copy-start.19 = (f32[1536]{0:T(1024)S(1)}, f32[1536]{0:T(1024)}, u32[]{:S(2)}) copy-start(f32[1536]{0:T(1024)} %copy-done.18) | copy-start | bytes 18436
  480.2 115.1 %copy-start.21 = (f32[512]{0:T(512)S(1)}, f32[512]{0:T(512)}, u32[]{:S(2)}) copy-start(f32[512]{0:T(512)} %copy-done.20) | copy-start | bytes 6148
  595.3 6.2 copy-start.3
  595.3 6.2 copy-start.9
  595.4 7.2 slice-start
  602.7 3.7 copy-start.7
  606.5 38.5 %copy-start.11 = (bf16[1,512,1536]{2,1,0:T(8,128)(2,1)S(1)}, bf16[1,512,1536]{2,1,0:T(8,128)(2,1)}, u32[]{:S(2)}) copy-start(bf16[1,512,1536]{2,1,0:T(8,128)(2,1)} %param.11) | copy-start | bytes 4718596
  606.5 38.5 %copy-start.23 = (f32[1536]{0:T(1024)S(1)}, f32[1536]{0:T(1024)}, u32[]{:S(2)}) copy-start(f32[1536]{0:T(1024)} %copy-done.22) | copy-start | bytes 18436
  606.5 38.5 %copy-start.26 = (f32[512]{0:T(512)S(1)}, f32[512]{0:T(512)}, u32[]{:S(2)}) copy-start(f32[512]{0:T(512)} %copy-done.25) | copy-start | bytes 6148
  645.0 11.1 %copy-start.5 = (bf16[512,1536]{1,0:T(8,128)(2,1)S(1)}, bf16[512,1536]{1,0:T(8,128)(2,1)}, u32[]{:S(2)}) copy-start(bf16[512,1536]{1,0:T(8,128)(2,1)} %copy-done.4) | copy-start | bytes 4718596
  657.2 10.4 %copy-start.8 = (f32[512,1536]{1,0:T(8,128)S(1)}, f32[512,1536]{1,0:T(8,128)}, u32[]{:S(2)}) copy-start(f32[512,1536]{1,0:T(8,128)} %copy-done.7) | copy-start | bytes 9437188
  657.2 10.4 %copy-start.27 = (bf16[512,1536]{1,0:T(8,128)(2,1)S(1)}, bf16[512,1536]{1,0:T(8,128)(2,1)}, u32[]{:S(2)}) copy-start(bf16[512,1536]{1,0:T(8,128)(2,1)} %get-tuple-element.28) | copy-start | bytes 4718596
  854.7 3.2 copy-start.6
  854.7 6.0 copy-start.17
  858.7 3.8 copy-start.15
  862.5 12.2 %copy-start.1 = (bf16[384,1536]{1,0:T(8,128)(2,1)S(1)}, bf16[384,1536]{1,0:T(8,128)(2,1)}, u32[]{:S(2)}) copy-start(bf16[384,1536]{1,0:T(8,128)(2,1)} %param.16) | copy-start | bytes 3538948
  (3 other events, 4.1 us)
Sparse Core Ops, SparseCore 0:
  11.5 80.8 all-gather.3
  94.3 85.9 all-gather.7
  182.2 52.0 all-gather.5
  473.6 69.0 reduce-scatter.4
  546.1 107.3 reduce-scatter.2

commit v3 on v2

--- a/solution.py
+++ b/solution.py
@@ -139,49 +139,6 @@
             @pl.when((behind >= step) & (behind < owners - 1))
             def _():
                 copy(step).wait_send()
-
-
-def line_gather(blocks, owners, collective):
-    count = len(blocks)
-
-    def kernel(*refs):
-        own, outs = refs[:count], refs[count : 2 * count]
-        send, recv, local = refs[2 * count :]
-        me = lax.axis_index("expert")
-        greet_all(me, owners, 0, 0)
-        lines, copies = [], []
-        for i in range(count):
-
-            def source_of(step, origin, i=i):
-                return own[i] if step == 0 else outs[i].at[origin]
-
-            def target_of(origin, i=i):
-                return outs[i].at[origin]
-
-            lines.append(line_sends(me, owners, source_of, target_of, send, recv, i))
-        for step in range(owners):
-            for i in range(count):
-                line_step(step, lines[i], owners)
-            if step == 0:
-                for i in range(count):
-                    copies.append(pltpu.make_async_copy(own[i], outs[i].at[me], local.at[i]))
-                    copies[-1].start()
-        for i in range(count):
-            copies[i].wait()
-            line_finish(lines[i], owners)
-
-    return pl.pallas_call(
-        kernel,
-        out_shape=[jax.ShapeDtypeStruct((owners,) + b.shape, b.dtype) for b in blocks],
-        in_specs=[vmem_spec()] * count,
-        out_specs=[any_spec()] * count,
-        scratch_shapes=[
-            pltpu.SemaphoreType.DMA((count, 2, owners - 1)),
-            pltpu.SemaphoreType.DMA((count, 2, owners - 1)),
-            pltpu.SemaphoreType.DMA((count,)),
-        ],
-        compiler_params=kernel_params(collective),
-    )(*blocks)
 
 
 def add_rows(target, addend, chunk):
@@ -273,7 +230,8 @@
         lines = []
         for i in range(count):
             held, send, recv = scratch[3 * i : 3 * i + 3]
-            lines.append(scatter_line(own[i], held, outs[i], send, recv, me, owners, 32))
+            chunk = math.gcd(32, own[i].shape[1])
+            lines.append(scatter_line(own[i], held, outs[i], send, recv, me, owners, chunk))
         for step in range(owners - 1):
             for advance, _ in lines:
                 advance(step)
@@ -809,6 +767,219 @@
     )(length, projected, cosine, sine, stream)
 
 
+def visit_of(visit, me, owners):
+    left, right = me, owners - 1 - me
+    both = jnp.minimum(left, right)
+    paired = visit <= 2 * both
+    distance = jnp.where(paired, (visit + 1) // 2, visit - both)
+    odd = lax.rem(visit, 2) == 1
+    toward_left = jnp.where(paired, odd, left > right)
+    opens = jnp.where(paired, odd, True) & (visit > 0)
+    source = jnp.where(toward_left, me - distance, me + distance)
+    return jnp.where(visit == 0, me, source), distance, opens
+
+
+def expert_pass(rows, extra, upstream, inner, down, owners, capacity, collective):
+    length, width = rows.shape
+    count, _, wide = inner.shape
+    hidden_width = wide // 2
+    experts = count * owners
+    places = -(-capacity // 16) * 16
+    gate_rows = -(-experts // 8) * 8
+
+    def kernel(
+        rows_ref, extra_ref, upstream_ref, inner_ref, down_ref,
+        all_ref, rows_out, grad_out, gate_out, hidden_out, back_out, mixed_out, slope_ref,
+        inner_v, down_v, block_v, grad_v, table, table_wide, picks, dx, yw,
+        rows_s, grad_s, gate_s, hidden_s, back_s, mixed_s,
+        line_send, line_recv, weight_sem, load_sem, save_sem, sum_sem, own_sem,
+    ):
+        me = lax.axis_index("expert")
+        greet_all(me, owners, 0, 0)
+        sources = ((extra_ref, table), (rows_ref, all_ref))
+        lines = []
+        for slot, (first, rest) in enumerate(sources):
+
+            def source_of(step, origin, first=first, rest=rest):
+                return first if step == 0 else rest.at[origin]
+
+            lines.append(
+                line_sends(
+                    me, owners, source_of, lambda origin, rest=rest: rest.at[origin],
+                    line_send, line_recv, slot,
+                )
+            )
+        own = [
+            pltpu.make_async_copy(first, rest.at[me], own_sem.at[slot])
+            for slot, (first, rest) in enumerate(sources)
+        ]
+        for one in own:
+            one.start()
+        for sides in lines:
+            line_step(0, sides, owners)
+
+        def weights(e):
+            return (
+                pltpu.make_async_copy(inner_ref.at[e], inner_v.at[e], weight_sem.at[0, e]),
+                pltpu.make_async_copy(down_ref.at[e], down_v.at[e], weight_sem.at[1, e]),
+            )
+
+        for e in range(count):
+            for one in weights(e):
+                one.start()
+        slope_ref[...] = jnp.zeros(slope_ref.shape, F32)
+        for one in own:
+            one.wait()
+
+        def saves(source, e, half):
+            at = pl.ds(pl.multiple_of(source * places, 16), places)
+            return [
+                pltpu.make_async_copy(s.at[half], o.at[e, at], save_sem.at[i, half])
+                for i, (s, o) in enumerate(
+                    ((rows_s, rows_out), (grad_s, grad_out), (gate_s, gate_out), (hidden_s, hidden_out))
+                )
+            ]
+
+        def sums(source):
+            return [
+                pltpu.make_async_copy(s, o.at[source], sum_sem.at[i])
+                for i, (s, o) in enumerate(((back_s, back_out), (mixed_s, mixed_out)))
+            ]
+
+        @pl.loop(0, owners)
+        def _(visit):
+            source, distance, opens = visit_of(visit, me, owners)
+            for step in range(1, owners):
+
+                @pl.when(opens & (distance == step))
+                def _():
+                    for sides in lines:
+                        line_step(step, sides, owners)
+
+            loads = (
+                pltpu.make_async_copy(all_ref.at[source], block_v, load_sem.at[0]),
+                pltpu.make_async_copy(upstream_ref.at[source], grad_v, load_sem.at[1]),
+            )
+            for one in loads:
+                one.start()
+            table_wide[...] = table[source].astype(F32)
+            for one in loads:
+                one.wait()
+
+            @pl.loop(0, count)
+            def _(e):
+                half = lax.rem(e, 2)
+                expert = me * count + e
+                slot = table_wide[pl.ds(expert, 1), :]
+                weight = (
+                    table_wide[pl.ds(experts + expert, 1), :]
+                    + table_wide[pl.ds(2 * experts + expert, 1), :]
+                )
+                place = lax.broadcasted_iota(jnp.int32, (places, length), 0).astype(F32)
+                hits = place == slot
+                pick = hits.astype(BF16)
+                column = jnp.sum(jnp.where(hits, weight, 0.0), -1, keepdims=True)
+                at = pl.ds(pl.multiple_of(e * places, 16), places)
+                picks[at, :] = pick
+
+                @pl.when(visit == 0)
+                def _():
+                    for one in weights(e):
+                        one.wait()
+
+                @pl.when((visit > 0) | (e >= 2))
+                def _():
+                    for one in saves(source, e, half):
+                        one.wait()
+
+                row = contract(pick, block_v[...], 1, 0).astype(BF16)
+                rows_s[half] = row
+                grad = contract(pick, grad_v[...], 1, 0).astype(BF16)
+                grad_s[half] = grad
+                gate_up = contract(row, inner_v[e], 1, 0)
+                slope = contract(grad, down_v[e], 1, 1)
+                gate, up = gate_up[:, :hidden_width], gate_up[:, hidden_width:]
+                sigmoid = 1.0 / (1.0 + jnp.exp(-gate))
+                active = gate * sigmoid
+                hidden = active * up
+                gate_slope = jnp.sum(hidden * slope, -1, keepdims=True)
+                slope_ref[source, pl.ds(expert, 1), :] = jnp.sum(
+                    jnp.where(hits, gate_slope, 0.0), 0, keepdims=True
+                )
+                hidden = (hidden * column).astype(BF16)
+                hidden_s[half] = hidden
+                slope = slope * column
+                gate_s[half, :, :hidden_width] = (
+                    slope * up * sigmoid * (1.0 + gate * (1.0 - sigmoid))
+                ).astype(BF16)
+                gate_s[half, :, hidden_width:] = (slope * active).astype(BF16)
+                dx[at, :] = contract(gate_s[half], inner_v[e], 1, 1).astype(BF16)
+                yw[at, :] = contract(hidden, down_v[e], 1, 0).astype(BF16)
+                for one in saves(source, e, half):
+                    one.start()
+
+            @pl.when(visit > 0)
+            def _():
+                for one in sums(source):
+                    one.wait()
+
+            back_s[...] = contract(picks[...], dx[...], 0, 0).astype(BF16)
+            mixed_s[...] = contract(picks[...], yw[...], 0, 0).astype(BF16)
+            for one in sums(source):
+                one.start()
+
+        for one in sums(0):
+            one.wait()
+        for half in range(2):
+            for one in saves(0, 0, half):
+                one.wait()
+        for sides in lines:
+            line_finish(sides, owners)
+
+    total = owners * places
+    shapes = [
+        ((owners, length, width), BF16),
+        ((count, total, width), BF16),
+        ((count, total, width), BF16),
+        ((count, total, wide), BF16),
+        ((count, total, hidden_width), BF16),
+        ((owners, length, width), BF16),
+        ((owners, length, width), BF16),
+        ((owners, gate_rows, length), F32),
+    ]
+    return pl.pallas_call(
+        kernel,
+        out_shape=[jax.ShapeDtypeStruct(*shape) for shape in shapes],
+        in_specs=[vmem_spec()] * 2 + [any_spec()] * 3,
+        out_specs=[any_spec()] * 7 + [vmem_spec()],
+        scratch_shapes=[
+            pltpu.VMEM(inner.shape, BF16),
+            pltpu.VMEM(down.shape, BF16),
+            pltpu.VMEM((length, width), BF16),
+            pltpu.VMEM((length, width), BF16),
+            pltpu.VMEM((owners, AUX, length), BF16),
+            pltpu.VMEM((AUX, length), F32),
+            pltpu.VMEM((count * places, length), BF16),
+            pltpu.VMEM((count * places, width), BF16),
+            pltpu.VMEM((count * places, width), BF16),
+            pltpu.VMEM((2, places, width), BF16),
+            pltpu.VMEM((2, places, width), BF16),
+            pltpu.VMEM((2, places, wide), BF16),
+            pltpu.VMEM((2, places, hidden_width), BF16),
+            pltpu.VMEM((length, width), BF16),
+            pltpu.VMEM((length, width), BF16),
+            pltpu.SemaphoreType.DMA((2, 2, owners - 1)),
+            pltpu.SemaphoreType.DMA((2, 2, owners - 1)),
+            pltpu.SemaphoreType.DMA((2, count)),
+            pltpu.SemaphoreType.DMA((2,)),
+            pltpu.SemaphoreType.DMA((4, 2)),
+            pltpu.SemaphoreType.DMA((2,)),
+            pltpu.SemaphoreType.DMA((2,)),
+        ],
+        compiler_params=kernel_params(collective),
+    )(rows, extra, upstream, inner, down)
+
+
 def gather_slow(piece, dp_index, dp_size):
     rows = piece.shape[0] // dp_size
     part = lax.dynamic_slice_in_dim(piece, dp_index * rows, rows, 0)
@@ -886,54 +1057,14 @@
     weight_high, weight_low = split_two(kept_weight)
     extra = jnp.concatenate(
         [slot_of, weight_high, weight_low, jnp.zeros((length, AUX - 3 * experts), BF16)], 1
-    )
-    rows_all, extra_all = line_gather([second_low, extra], owners, 2)
-    extra_all = extra_all.astype(F32)
-
-    def own(column):
-        return lax.dynamic_slice_in_dim(
-            extra_all, column * experts + owner * local_experts, local_experts, 2
-        )
-
-    slots = own(0)
-    weights_all = own(1) + own(2)
-    hits = slots.transpose(0, 2, 1)[:, :, None, :] == jnp.arange(capacity, dtype=F32)[:, None]
-    picks = hits.astype(BF16)
-    slot_weight = jnp.sum(
-        jnp.where(hits, weights_all.transpose(0, 2, 1)[:, :, None, :], 0.0), -1
-    )
+    ).T
+    down_full = lax.all_gather(expert_out, "dp", axis=1, tiled=True)
     inner_full = lax.all_gather(expert_in, "dp", axis=1, tiled=True)
-    down_full = lax.all_gather(expert_out, "dp", axis=1, tiled=True)
-    hidden_width = down_full.shape[1]
-
-    rows_in = dot("sect,std->escd", picks, rows_all).astype(BF16)
-    grad_in = dot("sect,std->escd", picks, upstream_all).astype(BF16)
-    gate_up = dot("escd,edf->escf", rows_in, inner_full)
-    gate_part = gate_up[..., :hidden_width]
-    up_part = gate_up[..., hidden_width:]
-    sigmoid_part = jax.nn.sigmoid(gate_part)
-    activated = gate_part * sigmoid_part
-    hidden = activated * up_part
-    weight_column = slot_weight.transpose(1, 0, 2)[..., None]
-    hidden_weighted = (hidden * weight_column).astype(BF16)
-    hidden_grad = dot("escd,ehd->esch", grad_in, down_full)
-    gate_grad_slot = jnp.sum(hidden.astype(BF16).astype(F32) * hidden_grad, -1)
-    hidden_grad = hidden_grad * weight_column
-    gate_part_grad = hidden_grad * up_part * sigmoid_part * (1.0 + gate_part * (1.0 - sigmoid_part))
-    up_grad = hidden_grad * activated
-    gate_up_grad = jnp.concatenate([gate_part_grad, up_grad], -1).astype(BF16)
-    row_grad = dot("escf,edf->escd", gate_up_grad, inner_full).astype(BF16)
-    back = dot("sect,escd->std", picks, row_grad).astype(BF16)
-    gate_grad_own = jnp.sum(
-        jnp.where(hits, gate_grad_slot.transpose(1, 0, 2)[..., None], 0.0), 2
-    ).transpose(0, 2, 1)
-    gate_wide = jnp.zeros((owners, length, experts), F32)
-    gate_wide = lax.dynamic_update_slice_in_dim(gate_wide, gate_grad_own, owner * local_experts, 2)
-    gate_packed = jnp.concatenate(
-        list(split_two(gate_wide)) + [jnp.zeros((owners, length, AUX - 2 * experts), BF16)], 2
-    )
-    inner_weight_grad = dot("escd,escf->edf", rows_in, gate_up_grad).astype(BF16)
-    down_weight_grad = dot("esch,escd->ehd", hidden_weighted, grad_in).astype(BF16)
+    _, rows_in, grad_in, gate_up_grad, hidden_weighted, back, mixed, slopes = expert_pass(
+        second_low, extra, upstream_all, inner_full, down_full, owners, capacity, 2
+    )
+    inner_weight_grad = dot("ecd,ecf->edf", rows_in, gate_up_grad).astype(BF16)
+    down_weight_grad = dot("ech,ecd->ehd", hidden_weighted, grad_in).astype(BF16)
     back, inner_weight_grad, down_weight_grad = lax.optimization_barrier(
         (back, inner_weight_grad, down_weight_grad)
     )
@@ -943,13 +1074,10 @@
     down_sum = lax.psum_scatter(
         down_weight_grad, "dp", scatter_dimension=1, tiled=True
     ).astype(F32)
-    back_sum, gate_sum = line_scatter([back, gate_packed], owners, 3)
-    back_sum, hidden_late = lax.optimization_barrier((back_sum, hidden_weighted))
-    expert_rows = dot("esch,ehd->escd", hidden_late, down_full).astype(BF16)
-    mixed = dot("sect,escd->std", picks, expert_rows).astype(BF16)
+    back_sum, slope_sum = line_scatter([back, slopes], owners, 3)
 
     upstream = cotangent[0].astype(F32) * live_rows
-    gate_grad = gate_sum[:, :experts] + gate_sum[:, experts : 2 * experts]
+    gate_grad = slope_sum[:experts].T
     logit_grad = gating * (gate_grad - jnp.sum(gating * gate_grad, -1, keepdims=True))
     second_grad = back_sum + jnp.dot(
         logit_grad, router_wide.T, precision=PRECISE

time: 890 us -> 823 us (0.925)
  matrix products: 219 us -> 91.8 us
  Pallas kernels: 578 us -> 626 us
  waiting for transfers between devices: 1.97 us -> 40.2 us
  other arithmetic: 41 us -> 21 us
    dot_general x16 -> x9, matrix products: 211 us -> 84.3 us  [dot(): return jnp.einsum(spec, a, b, preferred_element_type=F32)]
    pallas_call x1, Pallas kernels: 112 us -> 157 us  [expert_pass(): pl.pallas_call(kernel, out_shape=[jax.ShapeDtypeStruct(*shape) for shape...]
    all_gather x1, waiting for transfers between devices: 0.01 us -> 38.2 us  [per_device(): inner_full = lax.all_gather(expert_in, 'dp', axis=1, tiled=True)]
    another operation x1 -> x0, other arithmetic: 12.3 us -> none
  transfers between devices with their start and end apart: 5 -> 5, of which waited for: 0 -> 1; matrix products, arithmetic and copies ran while one was open for 19% -> 10% of each run, Pallas kernels for 66% -> 58%
where the time goes in v3:
time: 823 us; the launch traced here: 814 us
  Pallas kernels  626 us (76%)
  matrix products  91.8 us (11%)
  waiting for transfers between devices  40.2 us (5%)
  other arithmetic  21 us (3%)
  local copies, waits for them, and re-layouts  19.6 us (2%)
  between operations  15.3 us (2%)
    pallas_call x1, Pallas kernels, reduce_all(): pl.pallas_call(kernel, out_shape=[jax.ShapeDtypeStruct((2,) * bits + shap...  159 us
    pallas_call x1, Pallas kernels, expert_pass(): pl.pallas_call(kernel, out_shape=[jax.ShapeDtypeStruct(*shape) for shape...  157 us
    pallas_call x1, Pallas kernels, line_scatter(): pl.pallas_call(kernel, out_shape=[jax.ShapeDtypeStruct(b.shape[1:], F32)...  117 us
    pallas_call x1, Pallas kernels, gather_rows(): pl.pallas_call(kernel, out_shape=[jax.ShapeDtypeStruct(shape, BF16), jax....  116 us
    dot_general x9, matrix products, dot(): return jnp.einsum(spec, a, b, preferred_element_type=F32)  84.3 us
    pallas_call x1, Pallas kernels, attend_forward(): pl.pallas_call(kernel, out_shape=[jax.ShapeDtypeStruct((count, width), BF...  39.6 us
    all_gather x1, waiting for transfers between devices, per_device(): inner_full = lax.all_gather(expert_in, 'dp', axis=1, tiled=True)  38.2 us
    pallas_call x1, Pallas kernels, attend_backward(): pl.pallas_call(kernel, out_shape=jax.ShapeDtypeStruct((count, width + AUX...  38.1 us
  transfers between devices with their start and end apart: 5, of which 1 were waited for; matrix products, arithmetic and copies ran while one was open for 10% of the time, Pallas kernels for 58%

profile of v3, /device:TPU:0, one launch (start us, length us, event | category | flops | bytes accessed | tf_op | source)
XLA Modules:
  0.0 814.2 jit_solution(95207055476032386)
XLA Ops:
  7.3 1.2 copy-done
  12.0 3.0 concatenate.23.piece_ref
  15.0 116.1 %shard_map.178 = (bf16[4,2,2,2,48,2688]{5,4,3,2,1,0:T(8,128)(2,1)}, bf16[4,512,1536]{2,1,0:T(8,128)(2,1)}) custom-call(bf16[2,2,2,48,2688]{4,3,2,1,0:T(8,128)(2,1)} %concatenate.23.piece_ref, bf16[512,1536]{1,0:T(8,128)(2,1)} %bitcast.89), custom_call_target="tpu_custom_call" | custom-call | tf_op jit(solution)/shard_map/pallas_call | solution.py:537
  131.2 1.1 slice.37
  135.2 10.1 %fusion.19.projected_ref = f32[512,2688]{1,0:T(8,128)} fusion(bf16[1536,2688]{1,0:T(8,128)(2,1)} %bitcast.96, bf16[1,512,1536]{2,1,0:T(8,128)(2,1)S(1)} %copy-done.10, f32[1536]{0:T(1024)S(1)} %get-tuple-element.56, f32[512]{0:T(512)S(1)} %add_rsqrt_fusion.1), kind=kOutput, calls=%fused_computation.35 | convolution fusion | flops 4231004160 | bytes 15343616 | tf_op jit(solution)/shard_map/td,df->tf/dot_general | solution.py:46
  145.2 39.6 %shard_map.179 = (bf16[512,2560]{1,0:T(8,128)(2,1)}, bf16[512,1536]{1,0:T(8,128)(2,1)}, bf16[4,512,1536]{2,1,0:T(8,128)(2,1)}) custom-call(s32[1]{0:T(128)} %copy.66.length_ref, f32[512,2688]{1,0:T(8,128)} %fusion.19.projected_ref, f32[512,128]{1,0:T(8,128)} %copy.54.cosine_ref, f32[512,128]{1,0:T(8,128)} %copy.55.sine_ref, ...), custom_call_target="tpu_custom_call", output_to_operand_aliasing={{2}: (4, {})} | custom-call | tf_op jit(solution)/shard_map/pallas_call | solution.py:755
  185.3 6.8 multiply_reduce_fusion.2
  192.5 1.1 copy-done.2
  193.6 1.5 select_reduce_fusion
  196.0 38.2 %all-gather.6.cloned.1.call-done.inner_ref = bf16[5,1536,1024]{2,1,0:T(8,128)(2,1)} async-done(((bf16[5,192,1024]{2,1,0:T(8,128)(2,1)}), bf16[5,1536,1024]{2,1,0:T(8,128)(2,1)}) %all-gather.6.cloned.1.call-update) | async-done | bytes 15728656 | tf_op jit(solution)/shard_map/all_gather | solution.py:1062
  234.2 156.7 %shard_map.180 = (bf16[4,512,1536]{2,1,0:T(8,128)(2,1)}, bf16[5,832,1536]{2,1,0:T(8,128)(2,1)}, bf16[5,832,1536]{2,1,0:T(8,128)(2,1)}, bf16[5,832,1024]{2,1,0:T(...) custom-call(bf16[512,1536]{1,0:T(8,128)(2,1)} %copy-done.2, ...), custom_call_target="tpu_custom_call" | custom-call | tf_op jit(solution)/shard_map/pallas_call | solution.py:950
  390.9 23.9 %convolution_convert_fusion = bf16[5,1536,1024]{2,1,0:T(8,128)(2,1)} fusion(bf16[5,832,1536]{2,1,0:T(8,128)(2,1)} %get-tuple-element.35, bf16[5,832,1024]{2,1,0:T(8,128)(2,1)} %get-tuple-element.36), kind=kOutput, calls=%fused_computation | convolution fusion | flops 13094092800 | bytes 37027840 | tf_op jit(solution)/shard_map/ecd,ecf->edf/dot_general | solution.py:46
  414.8 15.9 %convolution_convert_fusion.3 = bf16[5,512,1536]{2,1,0:T(8,128)(2,1)} fusion(bf16[5,832,512]{2,1,0:T(8,128)(2,1)} %get-tuple-element.37, bf16[5,832,1536]{2,1,0:T(8,128)(2,1)} %get-tuple-element.38), kind=kOutput, calls=%fused_computation.3 | convolution fusion | flops 6547046400 | bytes 24903680 | tf_op jit(solution)/shard_map/ech,ecd->ehd/dot_general | solution.py:46
  431.9 116.6 %shard_map.181 = (f32[512,1536]{1,0:T(8,128)}, f32[24,512]{1,0:T(8,128)}) custom-call(bf16[4,512,1536]{2,1,0:T(8,128)(2,1)} %get-tuple-element.39.refs_0_, f32[4,24,512]{2,1,0:T(8,128)} %get-tuple-element.40.refs_1_), custom_call_target="tpu_custom_call" | custom-call | tf_op jit(solution)/shard_map/pallas_call | solution.py:241
  549.4 4.6 multiply_reduce_fusion
  554.0 1.0 broadcast_in_dim.62
  555.0 1.0 multiply_add_fusion
  556.1 3.8 convolution_convert_fusion.4.grad_ref
  559.9 38.1 %shard_map.182 = bf16[512,2688]{1,0:T(8,128)(2,1)} custom-call(s32[1]{0:T(128)} %copy.66.length_ref, bf16[512,2560]{1,0:T(8,128)(2,1)} %get-tuple-element.32.rotated_ref, bf16[512,1536]{1,0:T(8,128)(2,1)} %convolution_convert_fusion.4.grad_ref, f32[512,128]{1,0:T(8,128)} %copy.54.cosine_ref, f32[512,128]{1,0:T(8,128)} %copy.55.sine_ref), custom_call_target="tpu_custom_call" | custom-call | tf_op jit(solution)/shard_map/pallas_call | solution.py:723
  598.0 11.7 %fusion.9 = (f32[512]{0:T(512)}, bf16[1536]{0:T(1024)(128)(2,1)S(1)}, f32[512,1536]{1,0:T(8,128)}) fusion(bf16[1,512,1536]{2,1,0:T(8,128)(2,1)} %param.11, f32[1536]{0:T(1024)S(1)} %get-tuple-element.56, f32[512]{0:T(512)S(1)} %add_rsqrt_fusion.1, bf16[512,2688]{1,0:T(8,128)(2,1)} %shard_map.182, bf16[1536,2688]{1,0:T(8,128)(2,1)} %bitcast.99), kind=kOutput, calls=%fused_computation.16 | convolution fusion | flops 4233361408 | bytes 15741952 | tf_op jit(solution)/shard_map/tf,df->td/dot_general | solution.py:46
  610.7 1.4 convolution_convert_fusion.5
  612.1 1.1 copy.58
  613.3 7.2 convolution_convert_fusion.1
  621.1 4.7 convolution_convert_fusion.2
  625.8 158.8 %shard_map.183 = (bf16[2,2,2,48,2688]{4,3,2,1,0:T(8,128)(2,1)}, bf16[2,2,2,48,1536]{4,3,2,1,0:T(8,128)(2,1)}, f32[512,1536]{1,0:T(8,128)}) custom-call(bf16[4,2,2,2,48,2688]{5,4,3,2,1,0:T(8,128)(2,1)} %bitcast.88, bf16[4,2,2,2,48,1536]{5,4,3,2,1,0:T(8,128)(2,1)} %bitcast.90, bf16[4,512,1536]{2,1,0:T(8,128)(2,1)} %get-tuple-element.43.refs_2_), custom_call_target="tpu_custom_call" | custom-call | tf_op jit(solution)/shard_map/pallas_call | solution.py:446
  784.6 1.8 bitcast_convert_fusion
  786.5 2.7 slice.42
  790.5 2.1 slice_reduce_fusion
  792.5 3.0 bitcast_convert_fusion.1
  795.5 5.0 fusion.17
  800.5 2.8 convert_element_type.120
  803.3 3.9 convert_element_type.119
  (97 shorter events, 12.1 us)
Async XLA Ops:
  7.2 1.3 copy-start
  7.2 4.1 copy-start.15
  7.2 4.3 copy-start.18
  7.2 4.5 copy-start.19
  7.2 4.8 copy-start.11
  7.2 178.1 %all-gather.4.cloned.1.call-start = ((), (), s32[]{:S(2)}) async-start(), calls=%async_computation.2 | async-start | bytes 4866048 | tf_op jit(solution)/shard_map/all_gather | solution.py:986
  9.2 186.9 %all-gather.8.cloned.1.call-start = ((), (), s32[]{:S(2)}) async-start(), calls=%async_computation.4 | async-start | bytes 8847360 | tf_op jit(solution)/shard_map/all_gather | solution.py:1061
  9.9 224.3 %all-gather.6.cloned.1.call-start = ((), (), s32[]{:S(2)}) async-start(), calls=%async_computation.3 | async-start | bytes 17694720 | tf_op jit(solution)/shard_map/all_gather | solution.py:1062
  10.6 789.9 %reduce-scatter.5.cloned.1.call-start = ((), (), s32[]{:S(2)}) async-start(), calls=%async_computation.6 | async-start | bytes 8847360 | tf_op jit(solution)/shard_map/reduce_scatter | solution.py:1074
  131.2 3.6 copy-start.10
  145.2 39.7 %copy-start.16 = (s32[1,512,8]{1,2,0:T(8,128)S(1)}, s32[1,512,8]{1,2,0:T(8,128)}, u32[]{:S(2)}) copy-start(s32[1,512,8]{1,2,0:T(8,128)} %param.13) | copy-start | bytes 49156
  192.5 1.1 copy-start.2
  430.7 372.6 %reduce-scatter.3.cloned.1.call-start = ((), (), s32[]{:S(2)}) async-start(), calls=%async_computation.5 | async-start | bytes 17694720 | tf_op jit(solution)/shard_map/reduce_scatter | solution.py:1071
  549.4 5.7 copy-start.9
  549.4 6.7 slice-start
  555.0 1.1 slice-start.1
  556.1 3.8 copy-start.5
  598.0 12.7 %copy-start.3 = (bf16[512,1536]{1,0:T(8,128)(2,1)S(1)}, bf16[512,1536]{1,0:T(8,128)(2,1)}, u32[]{:S(2)}) copy-start(bf16[512,1536]{1,0:T(8,128)(2,1)} %copy-done.2) | copy-start | bytes 4718596
  598.0 12.8 %copy-start.14 = (f32[24,512]{1,0:T(8,128)S(1)}, f32[24,512]{1,0:T(8,128)}, u32[]{:S(2)}) copy-start(f32[24,512]{1,0:T(8,128)} %get-tuple-element.42) | copy-start | bytes 147460
  613.3 7.3 copy-start.12
  613.3 7.3 copy-start.13
  613.3 7.3 copy-start.20
  613.3 7.8 copy-start.6
  613.3 7.8 copy-start.21
  621.1 4.7 copy-start.8
  786.5 3.2 copy-start.4
  786.5 6.0 copy-start.17
  790.5 5.0 copy-start.7
  800.5 6.7 copy-start.1
Sparse Core Ops, SparseCore 0:
  11.5 80.3 all-gather.3
  93.8 53.1 all-gather.7
  148.9 85.2 all-gather.5
  430.8 67.3 reduce-scatter.4
  501.6 107.4 reduce-scatter.2
